TPU v7x, 32 devices: a whole 2x2x4 slice. The times are simulated.
32 devices in a mesh: expert: 8 (over z, y), tensor: 4 (over x, core).
Axes of the slice: x: 2, y: 2, z: 4, core: 2. Of those that a mesh axis runs over, the one named last changes fastest.
Arguments:
- block_input: bfloat16 [8192, 2048], P('expert', 'tensor'), may hold values from -6 to 6
- cotangent: bfloat16 [8192, 2048], P('expert', 'tensor'), may hold values from -6 to 6
- lengths: int32 [8], P('expert'), may hold values from 256 to 1024, as said below
- routes: int32 [8192, 8], P('expert'), may hold values from 0 to 15, all different within a row; in each aligned block of 1024 rows (0 to 1023, 1024 to 2047, ...) at most 576 rows name the same one
- g_attn: float32 [2048], replicated, may hold values from 0.5 to 1.5
- w_query: bfloat16 [2048, 2048], P(None, 'tensor'), may hold values from -0.125 to 0.125
- w_key: bfloat16 [2048, 2048], P(None, 'tensor'), may hold values from -0.125 to 0.125
- w_value: bfloat16 [2048, 2048], P(None, 'tensor'), may hold values from -0.125 to 0.125
- g_query: float32 [2048], P('tensor'), may hold values from 0.5 to 1.5
- g_key: float32 [2048], P('tensor'), may hold values from 0.5 to 1.5
- w_out: bfloat16 [2048, 2048], P('tensor'), may hold values from -0.5 to 0.5
- g_moe: float32 [2048], replicated, may hold values from 0.5 to 1.5
- w_router: bfloat16 [2048, 16], replicated, may hold values from -0.125 to 0.125
- w_gate: bfloat16 [16, 2048, 1024], P('expert', None, 'tensor'), may hold values from -0.125 to 0.125
- w_up: bfloat16 [16, 2048, 1024], P('expert', None, 'tensor'), may hold values from -0.125 to 0.125
- w_down: bfloat16 [16, 1024, 2048], P('expert', 'tensor'), may hold values from -6 to 6
Outputs:
- output: bfloat16 [8192, 2048], P('expert', 'tensor')
- grad_input: bfloat16 [8192, 2048], P('expert', 'tensor')
- grad_g_attn: float32 [2048], replicated
- grad_w_query: float32 [2048, 2048], P(None, 'tensor')
- grad_w_key: float32 [2048, 2048], P(None, 'tensor')
- grad_w_value: float32 [2048, 2048], P(None, 'tensor')
- grad_g_query: float32 [2048], P('tensor')
- grad_g_key: float32 [2048], P('tensor')
- grad_w_out: float32 [2048, 2048], P('tensor')
- grad_g_moe: float32 [2048], replicated
- grad_w_router: float32 [2048, 16], replicated
- grad_w_gate: float32 [16, 2048, 1024], P('expert', None, 'tensor')
- grad_w_up: float32 [16, 2048, 1024], P('expert', None, 'tensor')
- grad_w_down: float32 [16, 1024, 2048], P('expert', 'tensor')
Inputs may be any that keep to these rules, and one draw needn't show every extreme that they name: `lengths`: some slot has length 1024 and some has length 256. `routes`: the 8 experts of a token differ; among the rows of one device (aligned blocks of 1024 rows) no expert is named more than 576 times, a bound that some block reaches.
All inputs are finite; a program needn't handle non-finite values.
Results may differ from a plain program's by a relative error of at most 0.028.
Values may be sent and summed in bfloat16 or wider, within the bound.
No kernel may reach another device: no remote copies, remote signals or barrier semaphores. Data moves between devices by JAX's collectives and lax.ppermute only.
A program may use at most 576 MiB of HBM per device.

v0:
```python
import functools

import jax
import jax.numpy as jnp
from jax import lax
from jax.experimental import pallas as pl
from jax.experimental.pallas import tpu as pltpu
from jax.sharding import PartitionSpec as P


HD = 128
SLOT = 1024


EPS = 1e-05
THETA = 10000.0
NEGATIVE = -1e30


def cross_dot(operand, other_side):
    return lax.dot_general(
        operand, other_side, (((0,), (0,)), ((), ())), preferred_element_type=jnp.float32
    )


def dot_transposed(operand, other_side):
    return lax.dot_general(
        operand, other_side, (((1,), (1,)), ((), ())), preferred_element_type=jnp.float32
    )


def rotary_tables(length, head_size):
    frequency = THETA ** (-jnp.arange(0, head_size // 2, dtype=jnp.float32) * 2.0 / head_size)
    angles = jnp.arange(length, dtype=jnp.float32)[:, None] * frequency[None, :]
    return (jnp.cos(angles)[:, None, :], jnp.sin(angles)[:, None, :])


def rotate(values, cosine, sine_table):
    half_size = values.shape[-1] // 2
    first_half = values[..., :half_size]
    second = values[..., half_size:]
    return jnp.concatenate(
        [first_half * cosine - second * sine_table, second * cosine + first_half * sine_table],
        axis=-1,
    )


def unrotate(gradient, cosine, sine_table):
    half_size = gradient.shape[-1] // 2
    first_half = gradient[..., :half_size]
    second = gradient[..., half_size:]
    return jnp.concatenate(
        [first_half * cosine + second * sine_table, second * cosine - first_half * sine_table],
        axis=-1,
    )


def head_probs(q_ref, k_ref, length, start, stop):
    scores = dot_transposed(q_ref[start:stop, :], k_ref[:stop, :]) * HD ** (-0.5)
    query_pos = start + lax.broadcasted_iota(jnp.int32, scores.shape, 0)
    key_pos = lax.broadcasted_iota(jnp.int32, scores.shape, 1)
    allowed = (key_pos <= query_pos) & (key_pos < length)
    scores = jnp.where(allowed, scores, NEGATIVE)
    terms = jnp.exp(scores - jnp.max(scores, axis=1, keepdims=True))
    return terms / jnp.sum(terms, axis=1, keepdims=True)


def attend_body(length, q_ref, k_ref, v_ref, out_ref):
    rows = q_ref.shape[0]
    tile = rows // 4
    for start in range(0, rows, tile):
        stop = start + tile
        probs = head_probs(q_ref, k_ref, length[0], start, stop).astype(jnp.bfloat16)
        out_ref[start:stop, :] = jnp.dot(
            probs, v_ref[:stop, :], preferred_element_type=jnp.float32
        ).astype(jnp.bfloat16)


def attend_back_body(length, q_ref, k_ref, v_ref, d_ref, dq_ref, dk_ref, dv_ref, dv_sum):
    rows = q_ref.shape[0]
    tile = rows // 4
    for start in range(rows - tile, -1, -tile):
        stop = start + tile
        probs = head_probs(q_ref, k_ref, length[0], start, stop)
        d_block = d_ref[start:stop, :]
        d_probs = dot_transposed(d_block, v_ref[:stop, :])
        spread = jnp.sum(probs * d_probs, axis=1, keepdims=True)
        d_scores = (HD ** (-0.5) * probs * (d_probs - spread)).astype(jnp.bfloat16)
        dq_ref[start:stop, :] = jnp.dot(
            d_scores, k_ref[:stop, :], preferred_element_type=jnp.float32
        )
        d_keys = cross_dot(d_scores, q_ref[start:stop, :])
        d_values = cross_dot(probs.astype(jnp.bfloat16), d_block)
        if stop == rows:
            dk_ref[...] = d_keys
            dv_sum[...] = d_values
        else:
            dk_ref[:stop, :] += d_keys
            dv_sum[:stop, :] += d_values
    dv_ref[...] = dv_sum[...].astype(jnp.bfloat16)


def per_head(body, lengths, operands, out_types, scratch):
    rows, width = operands[0].shape
    block = pl.BlockSpec((rows, HD), lambda h, *_: (0, h))
    return pl.pallas_call(
        body,
        out_shape=[jax.ShapeDtypeStruct((rows, width), t) for t in out_types],
        grid_spec=pltpu.PrefetchScalarGridSpec(
            num_scalar_prefetch=1,
            grid=(width // HD,),
            in_specs=[block] * len(operands),
            out_specs=[block] * len(out_types),
            scratch_shapes=scratch,
        ),
    )(lengths, *operands)


def act_body(
    n_local,
    n_before,
    meta,
    x_near,
    x_far,
    g_near,
    g_far,
    info_ref,
    gate_up_own,
    gate_up_other,
    down_own,
    down_other,
    *rest,
):
    outs = rest[n_before:]
    out_refs, back_refs = outs[:2], outs[2:4]
    x_all, g_all, pre_own, pre_other, inner_own, inner_other, dgate_ref, staged = outs[4:]
    cols = x_near.shape[2]
    hidden = down_own.shape[0]
    width = hidden // n_local
    place = meta[0]

    def columns(core, across):
        return pl.ds(pl.multiple_of((place ^ (core + 2 * across)) * cols, cols), cols)

    def spread(pieces, target):
        for core in range(2):
            for across in range(2):
                target[:, columns(core, across)] = pieces[core][across]

    def collect(value, targets):
        staged[...] = value.astype(jnp.bfloat16)
        for core in range(2):
            for across in range(2):
                targets[core][across] = staged[:, columns(core, across)]

    spread((x_near, x_far), x_all)
    spread((g_near, g_far), g_all)
    live = meta[1] < meta[2 + pl.program_id(0)]

    @pl.when(live)
    def _():
        scale = info_ref[:, n_local : n_local + 1]
        dgate = [None] * n_local
        out, back = None, None
        for gate_up, down, pre_ref, inner_ref in (
            (gate_up_own, down_own, pre_own, inner_own),
            (gate_up_other, down_other, pre_other, inner_other),
        ):
            pre = jnp.dot(x_all[...], gate_up[...], preferred_element_type=jnp.float32)
            d_raw = dot_transposed(g_all[...], down[...])
            for e in range(n_local):
                at = slice(e * width, (e + 1) * width)
                up_at = slice(hidden + e * width, hidden + (e + 1) * width)
                gate_pre = pre[:, at] * scale
                up_pre = pre[:, up_at] * scale
                gate = info_ref[:, e : e + 1]
                sigma = jax.nn.sigmoid(gate_pre)
                silu_value = gate_pre * sigma
                inner = silu_value * up_pre
                raw = d_raw[:, at]
                share = jnp.sum(inner * raw, axis=1, keepdims=True)
                dgate[e] = share if dgate[e] is None else dgate[e] + share
                d_inner = raw * (gate * scale)
                inner_ref[:, at] = (inner * gate).astype(jnp.bfloat16)
                pre_ref[:, at] = (
                    d_inner * up_pre * sigma * (1.0 + gate_pre * (1.0 - sigma))
                ).astype(jnp.bfloat16)
                pre_ref[:, up_at] = (d_inner * silu_value).astype(jnp.bfloat16)
            out_part = jnp.dot(inner_ref[...], down[...], preferred_element_type=jnp.float32)
            back_part = dot_transposed(pre_ref[...], gate_up[...])
            out = out_part if out is None else out + out_part
            back = back_part if back is None else back + back_part
        for e in range(n_local):
            dgate_ref[:, e : e + 1] = dgate[e]
        collect(out, out_refs)
        collect(back, back_refs)

    @pl.when(jnp.logical_not(live))
    def _():
        for ref in (pre_own, pre_other, inner_own, inner_other, dgate_ref):
            ref[...] = jnp.zeros_like(ref)
        for ref in (*out_refs, *back_refs):
            ref[...] = jnp.zeros_like(ref)


def act_call(step, n_steps, meta, x_pair, g_pair, info, weights, n_local, before):
    slots, pieces, rows, cols = x_pair[0].shape
    model = 2 * pieces * cols
    hidden = weights[2].shape[0]
    bf16 = jnp.bfloat16
    piece = pl.BlockSpec((None, pieces, rows, cols), lambda s, *_: (s, 0, 0, 0))
    g_piece = pl.BlockSpec((None, pieces, rows, cols), lambda s, *_: (s, 0, step, 0))
    info_rows = pl.BlockSpec((None, rows, info.shape[2]), lambda s, *_: (s, 0, 0))

    def stacked(minor):
        return pl.BlockSpec((None, None, rows, minor), lambda s, *_: (step, s, 0, 0))

    def whole(array):
        return pl.BlockSpec(array.shape, lambda s, *_: (0, 0), pipeline_mode=pl.Buffered(1))

    part = jax.ShapeDtypeStruct(x_pair[0].shape, bf16)
    minors = (model, model, 2 * hidden, 2 * hidden, hidden, hidden)
    stacks = tuple(jax.ShapeDtypeStruct((n_steps, slots, rows, m), bf16) for m in minors)
    results = pl.pallas_call(
        functools.partial(act_body, n_local, len(before)),
        out_shape=(part,) * 4 + stacks + (jax.ShapeDtypeStruct(info.shape, jnp.float32),),
        grid_spec=pltpu.PrefetchScalarGridSpec(
            num_scalar_prefetch=1,
            grid=(slots,),
            in_specs=[piece, piece, g_piece, g_piece, info_rows]
            + [whole(w) for w in weights]
            + [pl.BlockSpec(memory_space=pl.ANY)] * len(before),
            out_specs=[piece] * 4 + [stacked(m) for m in minors] + [info_rows],
            scratch_shapes=[pltpu.VMEM((rows, model), bf16)],
        ),
        input_output_aliases={10 + i: 4 + i for i in range(len(before))},
        name="experts",
    )(meta, *x_pair, *g_pair, info, *weights, *before)
    return results[:2], results[2:4], results[4:10], results[10]


def layer(
    block_input,
    cotangent,
    lengths,
    routes,
    g_attn,
    w_query,
    w_key,
    w_value,
    g_query,
    g_key,
    w_out,
    g_moe,
    w_router,
    w_gate,
    w_up,
    w_down,
):
    tok_rows, slice_width = block_input.shape
    n_tensor = lax.axis_size("tensor")
    n_expert = lax.axis_size("expert")
    model_width = slice_width * n_tensor
    n_experts = w_router.shape[1]
    n_local = w_gate.shape[0]
    heads_here = w_query.shape[1] // HD
    e_index = lax.axis_index("expert")
    offset = lax.axis_index("tensor") * slice_width
    t_index = lax.axis_index("tensor")
    x_index = t_index // 2
    n_steps = 2
    half = tok_rows // 2
    stripe = tok_rows // 8
    f32, bf16 = jnp.float32, jnp.bfloat16

    def over_core(v):
        return lax.ppermute(v, "tensor", [(i, i ^ 1) for i in range(n_tensor)])

    def over_x(v):
        return lax.ppermute(v, "tensor", [(i, i ^ 2) for i in range(n_tensor)])

    def over_y(v):
        return lax.ppermute(v, "expert", [(i, i ^ 1) for i in range(n_expert)])

    def over_z(v):
        return lax.ppermute(v, "expert", [(i, (i + 2) % n_expert) for i in range(n_expert)])

    def tensor_sum(v):
        v = v + over_core(v)
        return v + over_x(v)

    def striped(v, index):
        parts = v.reshape((-1, 2, stripe) + v.shape[1:])
        return lax.dynamic_index_in_dim(parts, index, 1, False).reshape((half,) + v.shape[1:])

    def unstriped(mine, other):
        shape = (-1, 1, stripe) + mine.shape[1:]
        a = jnp.where(x_index == 0, mine, other).reshape(shape)
        b = jnp.where(x_index == 0, other, mine).reshape(shape)
        return jnp.concatenate([a, b], axis=1).reshape((tok_rows,) + mine.shape[1:])

    def exchanged(rows):
        return jnp.stack([striped(rows, x_index), over_x(striped(rows, 1 - x_index))])

    def joined(parts):
        near, far = parts
        return (near.astype(f32) + over_core(far).astype(f32)).astype(bf16)

    def reduced(message):
        return lax.psum_scatter(message, "expert", scatter_dimension=0)

    def home(total):
        return unstriped(total[0].astype(f32), over_x(total[1]).astype(f32))

    def expert_sum(grad):
        rows, cols = grad.shape
        n_z, z_index, y_index = n_expert // 2, e_index // 2, e_index % 2
        parts = grad.astype(bf16).reshape(2, n_z, rows // n_expert, cols)
        sent = over_y(lax.dynamic_index_in_dim(parts, 1 - y_index, 0, False))
        kept = lax.dynamic_index_in_dim(parts, y_index, 0, False)
        kept = kept.astype(f32) + sent.astype(f32)
        carried = None
        for step in [*range(1, n_z), 0]:
            at = lax.rem(z_index + n_z - step, n_z)
            total = lax.dynamic_index_in_dim(kept, at, 0, False)
            if carried is not None:
                total = total + carried.astype(f32)
            if step:
                carried = over_z(total.astype(bf16))
        near = [total.astype(bf16)]
        for _ in range(1, n_z):
            near.append(over_z(near[-1]))
        far = [over_y(v) for v in near]

        def ordered(pieces):
            pieces = pieces[::-1]
            doubled = jnp.concatenate(pieces + pieces[:-1], axis=0)
            start = (n_z - 1 - z_index) * (rows // n_expert)
            return lax.dynamic_slice_in_dim(doubled, start, rows // 2, 0)

        near, far = ordered(near), ordered(far)
        first = y_index == 0
        return jnp.concatenate(
            [jnp.where(first, near, far), jnp.where(first, far, near)], axis=0
        ).astype(f32)

    def column_parts(make):
        p0, p1, p2, p3 = [make((t_index ^ p) * slice_width) for p in range(4)]
        mine = p0 + over_core(p1.astype(bf16)).astype(f32)
        other = p2 + over_core(p3.astype(bf16)).astype(f32)
        return mine + over_x(other.astype(bf16)).astype(f32)

    def own_columns(vector):
        return lax.dynamic_slice_in_dim(vector, offset, slice_width, vector.ndim - 1)

    full_input = lax.all_gather(block_input, "tensor", axis=1, tiled=True)
    own_gu = jnp.concatenate(
        [w_gate[e] for e in range(n_local)] + [w_up[e] for e in range(n_local)], axis=1
    )
    own_down = w_down.reshape(-1, model_width)
    early_gu, early_down, early_dy, _ = lax.optimization_barrier(
        (own_gu, own_down, cotangent, full_input)
    )
    dy_near = lax.all_gather(exchanged(early_dy), "expert", axis=0)
    mats = (own_gu, over_x(early_gu), own_down, over_x(early_down))
    positions = jnp.arange(tok_rows)
    live_rows = positions < lengths[0]
    valid_rows = live_rows.astype(jnp.float32)[:, None]
    input_full = full_input.astype(jnp.float32)
    scale_x = lax.rsqrt(jnp.mean(input_full * input_full, axis=-1, keepdims=True) + EPS)
    normed = (input_full * scale_x * g_attn).astype(jnp.bfloat16)
    q_raw = jnp.dot(normed, w_query, preferred_element_type=jnp.float32)
    k_raw = jnp.dot(normed, w_key, preferred_element_type=jnp.float32)
    values = jnp.dot(normed, w_value, preferred_element_type=jnp.float32).astype(jnp.bfloat16)
    q_total, k_total = tensor_sum(
        jnp.stack([jnp.sum(q_raw * q_raw, axis=1), jnp.sum(k_raw * k_raw, axis=1)])
    )
    scale_q = lax.rsqrt(q_total / model_width + EPS)[:, None]
    scale_k = lax.rsqrt(k_total / model_width + EPS)[:, None]
    q_norm = q_raw * scale_q * g_query
    k_norm = k_raw * scale_k * g_key
    cosine, sine_table = rotary_tables(SLOT, HD)
    head_shape = (SLOT, heads_here, HD)
    flat_shape = (tok_rows, heads_here * HD)
    query = rotate(q_norm.reshape(head_shape), cosine, sine_table).astype(bf16).reshape(flat_shape)
    keys = rotate(k_norm.reshape(head_shape), cosine, sine_table).astype(bf16).reshape(flat_shape)
    (heads_out,) = per_head(attend_body, lengths, (query, keys, values), [bf16], [])
    attn_slice = column_parts(
        lambda at: jnp.dot(
            heads_out,
            lax.dynamic_slice_in_dim(w_out, at, slice_width, 1),
            preferred_element_type=f32,
        )
    )
    hidden = block_input.astype(f32) + attn_slice
    g_moe_slice = own_columns(g_moe)
    moe_rows = (hidden * g_moe_slice).astype(jnp.bfloat16)
    moe_piece = exchanged(moe_rows)
    moe_piece, dy_near = lax.optimization_barrier((moe_piece, dy_near))
    x_near = [
        lax.all_gather(v, "expert", axis=0) for v in jnp.split(moe_piece, n_steps, axis=1)
    ]
    router_slice = lax.dynamic_slice_in_dim(w_router, offset, slice_width, 0)
    statistics = jnp.concatenate(
        [
            jnp.dot(moe_rows, router_slice, preferred_element_type=jnp.float32),
            jnp.sum(hidden * hidden, axis=1, keepdims=True),
        ],
        axis=1,
    )
    statistics = tensor_sum(statistics.T).T
    scale_h = lax.rsqrt(statistics[:, n_experts:] / model_width + EPS)
    router_probs = jax.nn.softmax(statistics[:, :n_experts] * scale_h, axis=-1)
    expert_ids = jnp.arange(n_experts, dtype=jnp.int32)
    chosen = jnp.any(routes[:, :, None] == expert_ids[None, None, :], axis=1) & live_rows[:, None]
    chosen = chosen.astype(jnp.float32)
    gates = router_probs * chosen
    flat = jnp.concatenate(
        [
            gates.T,
            scale_h.T,
            jnp.full((1, tok_rows), lengths[0].astype(f32)),
            jnp.zeros((6, tok_rows), f32),
        ],
        axis=0,
    )
    flat = lax.all_gather(flat, "expert", axis=0)
    all_lengths = flat[:, n_experts + 1, 0].astype(jnp.int32)
    info = jnp.concatenate(
        [
            lax.dynamic_slice_in_dim(flat, e_index * n_local, n_local, 1),
            flat[:, n_experts : n_experts + 1],
            jnp.zeros((n_expert, 8 - n_local - 1, tok_rows), f32),
        ],
        axis=1,
    )
    info = lax.dynamic_index_in_dim(info.reshape(n_expert, 8, -1, 2, stripe), x_index, 3, False)
    info = info.reshape(n_expert, 8, n_steps, -1).transpose(2, 0, 3, 1)
    part_rows = half // n_steps

    dy_pair = (dy_near, over_core(dy_near))
    out_parts, back_parts, extras, stacks = [], [], [], ()
    for step in range(n_steps):
        first = step * 2 * part_rows + x_index * stripe
        meta = jnp.concatenate([jnp.stack([t_index, first]), all_lengths])
        x_pair = (x_near[step], over_core(x_near[step]))
        outs, backs, stacks, dgate = act_call(
            step, n_steps, meta, x_pair, dy_pair, info[step], mats, n_local, stacks
        )
        out_parts.append(outs)
        rows = lax.dynamic_update_slice_in_dim(
            jnp.zeros((n_expert, n_experts, slice_width), f32),
            jnp.pad(
                dgate[:, :, :n_local].transpose(0, 2, 1),
                ((0, 0), (0, 0), (0, slice_width - part_rows)),
            ),
            e_index * n_local,
            1,
        )
        high = lax.reduce_precision(rows, 8, 7)
        extra = jnp.stack([high, rows - high], axis=1).astype(bf16)
        total = reduced(jnp.concatenate([joined(backs), extra], axis=2))
        back_parts.append(total[:, :part_rows])
        extra = total[:, part_rows:, :part_rows].astype(f32)
        extras.append(extra[0] + extra[1])
    x_stack, g_stack, pre_own, pre_other, inner_own, inner_other = [
        v.reshape(-1, v.shape[3]) for v in stacks
    ]
    other_gu = cross_dot(x_stack, pre_other).astype(bf16)
    other_down = cross_dot(inner_other, g_stack).astype(bf16)
    mine_gu = cross_dot(x_stack, pre_own)
    mine_down = cross_dot(inner_own, g_stack)
    out_message = jnp.concatenate([joined(parts) for parts in out_parts], axis=2)
    back_total = jnp.concatenate(back_parts, axis=1)
    back_total, out_message, other_gu, other_down, mine_gu, mine_down = lax.optimization_barrier(
        (back_total, out_message, other_gu, other_down, mine_gu, mine_down)
    )
    back_slice = home(back_total)
    moe_total = reduced(out_message)

    total = jnp.concatenate(extras, axis=1)
    total = total + over_core(total)
    d_gates = unstriped(total.T, over_x(total).T)

    d_probs = d_gates * chosen
    d_logits = (
        router_probs * (d_probs - jnp.sum(router_probs * d_probs, axis=-1, keepdims=True))
    ).astype(jnp.bfloat16)
    scaled_logits = (d_logits.astype(jnp.float32) * scale_h).astype(jnp.bfloat16)
    router_grad = cross_dot(moe_rows, scaled_logits)
    back_slice = back_slice + dot_transposed(scaled_logits, router_slice)
    projection = jnp.sum(back_slice * (hidden * g_moe_slice), axis=1)
    h_term = (tensor_sum(projection[None])[0] / model_width)[:, None] * scale_h * scale_h
    d_out_slice = cotangent.astype(f32) * valid_rows
    d_hidden_slice = d_out_slice + g_moe_slice * back_slice - hidden * h_term
    grad_g_moe = jnp.sum(back_slice * hidden, axis=0)
    d_attn = d_hidden_slice.astype(bf16)
    across = over_x(d_attn)
    d_attn = [d_attn, over_core(d_attn), across, over_core(across)]
    grad_w_out = jnp.concatenate([cross_dot(heads_out, v) for v in d_attn], axis=1)
    d_heads = sum(
        dot_transposed(
            v, lax.dynamic_slice_in_dim(w_out, (t_index ^ p) * slice_width, slice_width, 1)
        )
        for p, v in enumerate(d_attn)
    )
    d_heads = d_heads.astype(bf16)
    other_gu, other_down, _ = lax.optimization_barrier((other_gu, other_down, d_attn[3]))
    other_gu, other_down = over_x(other_gu), over_x(other_down)
    d_query, d_keys, d_values = per_head(
        attend_back_body,
        lengths,
        (query, keys, values, d_heads),
        [f32, f32, bf16],
        [pltpu.VMEM((tok_rows, HD), f32)],
    )
    d_q_norm = unrotate(d_query.reshape(head_shape), cosine, sine_table).reshape(tok_rows, heads_here * HD)
    d_k_norm = unrotate(d_keys.reshape(head_shape), cosine, sine_table).reshape(tok_rows, heads_here * HD)
    q_sum, k_sum = tensor_sum(
        jnp.stack(
            [jnp.sum(d_q_norm * g_query * q_raw, axis=1), jnp.sum(d_k_norm * g_key * k_raw, axis=1)]
        )
    )
    grad_g_query = jnp.sum(d_q_norm * q_raw * scale_q, axis=0)
    grad_g_key = jnp.sum(d_k_norm * k_raw * scale_k, axis=0)
    d_q_raw = (
        scale_q * g_query * d_q_norm - q_raw * scale_q**3 * (q_sum / model_width)[:, None]
    ).astype(jnp.bfloat16)
    d_k_raw = (
        scale_k * g_key * d_k_norm - k_raw * scale_k**3 * (k_sum / model_width)[:, None]
    ).astype(jnp.bfloat16)
    grad_w_query = cross_dot(normed, d_q_raw)
    grad_w_key = cross_dot(normed, d_k_raw)
    grad_w_value = cross_dot(normed, d_values)

    def normed_columns(at):
        def back(gradient, weight):
            return dot_transposed(gradient, lax.dynamic_slice_in_dim(weight, at, slice_width, 0))

        return back(d_q_raw, w_query) + back(d_k_raw, w_key) + back(d_values, w_value)

    column_sums = jnp.sum(
        d_q_raw.astype(jnp.float32) * q_raw
        + d_k_raw.astype(jnp.float32) * k_raw
        + d_values.astype(jnp.float32) * values.astype(jnp.float32),
        axis=1,
    )
    x_mean = (tensor_sum(column_sums[None])[0] / model_width)[:, None]
    d_normed = column_parts(normed_columns)
    x_hat = block_input.astype(jnp.float32) * scale_x
    grad_g_attn = jnp.sum(d_normed * x_hat, axis=0)
    grad_input = (
        d_hidden_slice + scale_x * (d_normed * own_columns(g_attn) - x_hat * x_mean)
    ).astype(jnp.bfloat16)

    sum_query, sum_key, sum_value = map(expert_sum, (grad_w_query, grad_w_key, grad_w_value))
    ready, moe_total = lax.optimization_barrier((grad_w_out.astype(bf16), moe_total))
    sum_out = lax.psum(ready, "expert").astype(f32)
    moe_slice = home(moe_total)
    output = (valid_rows * (hidden + moe_slice)).astype(bf16)
    sum_out = jnp.concatenate(
        [
            lax.dynamic_slice_in_dim(sum_out, (t_index ^ p) * slice_width, slice_width, 1)
            for p in range(4)
        ],
        axis=1,
    )
    other_gu, other_down, _ = lax.optimization_barrier((other_gu, other_down, d_k_raw))
    grad_gu = mine_gu + other_gu.astype(f32)
    grad_w_down = (mine_down + other_down.astype(f32)).reshape(w_down.shape)
    grad_gu = grad_gu.reshape(model_width, 2, n_local, -1)
    grad_w_gate = grad_gu[:, 0].transpose(1, 0, 2)
    grad_w_up = grad_gu[:, 1].transpose(1, 0, 2)
    small = jnp.concatenate(
        [router_grad.T, grad_g_moe[None], grad_g_attn[None], grad_g_query[None], grad_g_key[None]],
        axis=0,
    )
    hop = 1
    while hop < n_expert:
        small = small + lax.ppermute(small, "expert", [(i, i ^ hop) for i in range(n_expert)])
        hop *= 2
    shared = tensor_sum(
        lax.dynamic_update_slice_in_dim(
            jnp.zeros((n_experts + 2, model_width), f32), small[: n_experts + 2], offset, 1
        )
    )
    return (
        output,
        grad_input,
        shared[n_experts + 1],
        sum_query,
        sum_key,
        sum_value,
        small[n_experts + 2],
        small[n_experts + 3],
        sum_out,
        shared[n_experts],
        shared[:n_experts].T,
        grad_w_gate,
        grad_w_up,
        grad_w_down,
    )


def solution(mesh):
    placed = (
        P("expert", "tensor"),
        P("expert", "tensor"),
        P("expert"),
        P("expert", None),
        P(),
        P(None, "tensor"),
        P(None, "tensor"),
        P(None, "tensor"),
        P("tensor"),
        P("tensor"),
        P("tensor", None),
        P(),
        P(),
        P("expert", None, "tensor"),
        P("expert", None, "tensor"),
        P("expert", "tensor", None),
    )
    return jax.shard_map(
        layer,
        mesh=mesh,
        in_specs=placed,
        out_specs=(
            P("expert", "tensor"),
            P("expert", "tensor"),
            P(),
            P(None, "tensor"),
            P(None, "tensor"),
            P(None, "tensor"),
            P("tensor"),
            P("tensor"),
            P("tensor", None),
            P(),
            P(),
            P("expert", None, "tensor"),
            P("expert", None, "tensor"),
            P("expert", "tensor", None),
        ),
        check_vma=False,
    )
```

profile of v0, /device:TPU:0, one launch (start us, length us, event | category | flops | bytes accessed | tf_op | source)
XLA Modules:
  0.0 1169.0 jit_solution(15050353168752204680)
XLA Ops:
  12.8 34.0 %all-gather.9.cloned.1.call-done = bf16[1024,2048]{1,0:T(8,128)(2,1)} async-done(((bf16[1024,512]{1,0:T(8,128)(2,1)}), bf16[1024,2048]{1,0:T(8,128)(2,1)}) %all-gather.9.cloned.1.call-update) | async-done | bytes 4194320 | tf_op jit(solution)/shard_map/all_gather | solution.py:356
  47.3 13.7 %collective-permute-done.8 = bf16[512,512]{1,0:T(8,128)(2,1)S(1)} collective-permute-done((bf16[512,512]{1,0:T(8,128)(2,1)S(1)}, bf16[512,512]{1,0:T(8,128)(2,1)S(1)}, u32[]{:S(2)}, u32[]{:S(2)}) %collective-permute-start.8) | collective-permute-done | bytes 524320 | tf_op jit(solution)/shard_map/ppermute | solution.py:280
  65.6 5.7 multiply_reduce_fusion.3
  78.4 6.3 convolution_convert_fusion.5.v_ref
  103.4 6.3 subtract_convert_fusion
  114.9 11.0 shard_map.263
  137.9 22.5 %collective-permute-done.4 = bf16[1024,512]{1,0:T(8,128)(2,1)} collective-permute-done((bf16[1024,512]{1,0:T(8,128)(2,1)}, bf16[1024,512]{1,0:T(8,128)(2,1)}, u32[]{:S(2)}, u32[]{:S(2)}) %collective-permute-start.4) | collective-permute-done | bytes 1048608 | tf_op jit(solution)/shard_map/ppermute | solution.py:280
  165.9 11.4 collective-permute-done.7
  178.3 8.4 all-gather.11.cloned.1.call-done
  190.6 69.8 %all-gather.13.cloned.1.call-done = bf16[16,256,512]{2,1,0:T(8,128)(2,1)} async-done(((bf16[2,256,512]{2,1,0:T(8,128)(2,1)}), bf16[16,256,512]{2,1,0:T(8,128)(2,1)}) %all-gather.13.cloned.1.call-update) | async-done | bytes 4194320 | tf_op jit(solution)/shard_map/all_gather | solution.py:401
  270.0 14.9 %collective-permute-done.6 = f32[17,1024]{1,0:T(8,128)S(1)} collective-permute-done((f32[17,1024]{1,0:T(8,128)S(1)}, f32[17,1024]{1,0:T(8,128)S(1)}, u32[]{:S(2)}, u32[]{:S(2)}) %collective-permute-start.6) | collective-permute-done | bytes 69664 | tf_op jit(solution)/shard_map/ppermute | solution.py:280
  285.2 34.9 %all-gather = f32[192,1024]{1,0:T(8,128)S(1)} all-gather(f32[24,1024]{1,0:T(8,128)S(1)} %maximum_maximum_fusion.2), channel_id=2, replica_groups=mesh['expert'=8,'tensor'=4] {'expert'}, dimensions={0}, use_global_device_ids=true | all-gather | bytes 884736 | tf_op jit(solution)/shard_map/all_gather | solution.py:427
  329.5 68.7 %experts.2 = (bf16[8,2,256,512]{3,2,1,0:T(8,128)(2,1)}, bf16[8,2,256,512]{3,2,1,0:T(8,128)(2,1)}, bf16[8,2,256,512]{3,2,1,0:T(8,128)(2,1)}, bf16[8,2,256,512]{3,...) custom-call(s32[10]{0:T(128)} %get-tuple-element.251.meta, ...), custom_call_target="tpu_custom_call" | custom-call | tf_op jit(solution)/shard_map/experts/pallas_call | solution.py:224
  413.1 51.2 %experts.3 = (bf16[8,2,256,512]{3,2,1,0:T(8,128)(2,1)}, bf16[8,2,256,512]{3,2,1,0:T(8,128)(2,1)}, bf16[8,2,256,512]{3,2,1,0:T(8,128)(2,1)}, bf16[8,2,256,512]{3,...) custom-call(s32[10]{0:T(128)} %get-tuple-element.252.meta, ...), custom_call_target="tpu_custom_call", output_to_operand_aliasing={{4}: (10, {}), {5}: (11, {}), {6}: (12, {}), {7}: (13, {}),... | custom-call | tf_op jit(solution)/shard_map/experts/pallas_call | solution.py:224
  469.0 24.0 %bitcast_convert_fusion = bf16[2048,1024]{1,0:T(8,128)(2,1)} fusion(bf16[2,8,256,2048]{3,2,1,0:T(8,128)(2,1)} %get-tuple-element.77, bf16[2,8,256,1024]{3,2,1,0:T(8,128)(2,1)} %get-tuple-element.78), kind=kOutput, calls=%fused_computation.6 | convolution fusion | flops 17181966336 | bytes 29360128 | tf_op jit(solution)/shard_map/dot_general | solution.py:21
  499.2 14.9 %bitcast_convert_fusion.1 = bf16[512,2048]{1,0:T(8,128)(2,1)} fusion(bf16[2,8,256,512]{3,2,1,0:T(8,128)(2,1)} %get-tuple-element.79, bf16[2,8,256,2048]{3,2,1,0:T(8,128)(2,1)} %get-tuple-element.80), kind=kOutput, calls=%fused_computation.19 | convolution fusion | flops 8590983168 | bytes 23068672 | tf_op jit(solution)/shard_map/dot_general | solution.py:21
  514.1 15.1 %convolution_bitcast_fusion.1 = f32[512,2048]{1,0:T(8,128)} fusion(bf16[2,8,256,512]{3,2,1,0:T(8,128)(2,1)} %get-tuple-element.82, bf16[2,8,256,2048]{3,2,1,0:T(8,128)(2,1)} %get-tuple-element.80), kind=kOutput, calls=%fused_computation.21 | convolution fusion | flops 8589934592 | bytes 25165824 | tf_op jit(solution)/shard_map/dot_general | solution.py:21
  529.2 21.3 %convolution_bitcast_fusion = f32[2048,1024]{1,0:T(8,128)} fusion(bf16[2,8,256,2048]{3,2,1,0:T(8,128)(2,1)S(1)} %bitcast.318, bf16[2,8,256,1024]{3,2,1,0:T(8,128)(2,1)S(1)} %bitcast.328), kind=kOutput, calls=%fused_computation.14 | convolution fusion | flops 17179869184 | bytes 33554432 | tf_op jit(solution)/shard_map/dot_general | solution.py:21
  550.5 7.2 add_convert_fusion.1
  557.7 5.7 add_convert_fusion
  563.4 7.6 pad_maximum_fusion
  573.5 24.9 %reduce-scatter.6.cloned.1.call-done = bf16[1,2,272,512]{3,2,1,0:T(8,128)(2,1)} async-done(((bf16[8,2,272,512]{3,2,1,0:T(8,128)(2,1)}), bf16[1,2,272,512]{3,2,1,0:T(8,128)(2,1)}) %reduce-scatter.6.cloned.1.call-update) | async-done | bytes 557072 | tf_op jit(solution)/shard_map/reduce_scatter | solution.py:310
  605.8 12.4 %collective-permute-done.18 = bf16[512,512]{1,0:T(8,128)(2,1)} collective-permute-done((bf16[512,512]{1,0:T(8,128)(2,1)}, bf16[512,512]{1,0:T(8,128)(2,1)}, u32[]{:S(2)}, u32[]{:S(2)}) %collective-permute-start.18) | collective-permute-done | bytes 524320 | tf_op jit(solution)/shard_map/ppermute | solution.py:280
  639.7 17.7 %collective-permute-done.24 = bf16[1024,512]{1,0:T(8,128)(2,1)} collective-permute-done((bf16[1024,512]{1,0:T(8,128)(2,1)}, bf16[1024,512]{1,0:T(8,128)(2,1)}, u32[]{:S(2)}, u32[]{:S(2)}) %collective-permute-start.24) | collective-permute-done | bytes 1048608 | tf_op jit(solution)/shard_map/ppermute | solution.py:280
  667.1 16.4 %shard_map.264 = (f32[1024,512]{1,0:T(8,128)}, f32[1024,512]{1,0:T(8,128)}, bf16[1024,512]{1,0:T(8,128)(2,1)}) custom-call(s32[1]{0:T(128)} %copy.289.length, bf16[1024,512]{1,0:T(8,128)(2,1)} %bitcast.320, bf16[1024,512]{1,0:T(8,128)(2,1)} %bitcast.322, bf16[1024,512]{1,0:T(8,128)(2,1)} %convolution_convert_fusion.5.v_ref, ...), custom_call_target="tpu_custom_call" | custom-call | tf_op jit(solution)/shard_map/pallas_call | solution.py:106
  712.8 35.6 %collective-permute-done.28 = f32[2,1024]{1,0:T(2,128)S(1)} collective-permute-done((f32[2,1024]{1,0:T(2,128)S(1)}, f32[2,1024]{1,0:T(2,128)S(1)}, u32[]{:S(2)}, u32[]{:S(2)}) %collective-permute-start.28) | collective-permute-done | bytes 8224 | tf_op jit(solution)/shard_map/ppermute | solution.py:280
  748.4 5.7 add_reduce_fusion
  776.2 16.9 %collective-permute-done.50 = bf16[4,256,512]{2,1,0:T(8,128)(2,1)S(1)} collective-permute-done((bf16[4,256,512]{2,1,0:T(8,128)(2,1)S(1)}, bf16[4,256,512]{2,1,0:T(8,128)(2,1)S(1)}, u32[]{:S(2)}, u32[]{:S(2)}) %collective-permute-start.50) | collective-permute-done | bytes 1048608 | tf_op jit(solution)/shard_map/ppermute | solution.py:283
  795.0 20.3 %collective-permute-done.39 = bf16[4,256,512]{2,1,0:T(8,128)(2,1)S(1)} collective-permute-done((bf16[4,256,512]{2,1,0:T(8,128)(2,1)S(1)}, bf16[4,256,512]{2,1,0:T(8,128)(2,1)S(1)}, u32[]{:S(2)}, u32[]{:S(2)}) %collective-permute-start.39) | collective-permute-done | bytes 1048608 | tf_op jit(solution)/shard_map/ppermute | solution.py:283
  821.5 9.2 collective-permute-done.40
  832.8 8.9 collective-permute-done.63
  849.6 7.0 collective-permute-done.52
  863.5 8.0 collective-permute-done.35
  873.3 12.7 %collective-permute-done.36 = f32[20,512]{1,0:T(8,128)S(1)} collective-permute-done((f32[20,512]{1,0:T(8,128)S(1)}, f32[20,512]{1,0:T(8,128)S(1)}, u32[]{:S(2)}, u32[]{:S(2)}) %collective-permute-start.36) | collective-permute-done | bytes 40992 | tf_op jit(solution)/shard_map/ppermute | solution.py:580
  889.7 6.1 collective-permute-done.43
  895.8 5.6 collective-permute-done.66
  901.4 36.9 %collective-permute-done.38 = f32[18,2048]{1,0:T(8,128)S(1)} collective-permute-done((f32[18,2048]{1,0:T(8,128)S(1)}, f32[18,2048]{1,0:T(8,128)S(1)}, u32[]{:S(2)}, u32[]{:S(2)}) %collective-permute-start.38) | collective-permute-done | bytes 147488 | tf_op jit(solution)/shard_map/ppermute | solution.py:280
  942.0 7.3 collective-permute-done.67
  958.1 8.1 collective-permute-done.56
  967.0 7.7 collective-permute-done.68
  976.9 6.9 collective-permute-done.71
  987.0 11.0 collective-permute-done.46
  1000.3 6.9 collective-permute-done.49
  1007.3 13.0 %collective-permute-done.57 = bf16[256,512]{1,0:T(8,128)(2,1)S(1)} collective-permute-done((bf16[256,512]{1,0:T(8,128)(2,1)S(1)}, bf16[256,512]{1,0:T(8,128)(2,1)S(1)}, u32[]{:S(2)}, u32[]{:S(2)}) %collective-permute-start.57) | collective-permute-done | bytes 262176 | tf_op jit(solution)/shard_map/ppermute | solution.py:283
  1020.9 5.7 collective-permute-done.60
  1033.0 6.9 convert_add_fusion
  1039.8 11.7 %reshape.304 = f32[2048,2,2,256]{3,2,1,0:T(2,128)} reshape(f32[2048,1024]{1,0:T(8,128)} %convert_add_fusion) | data formatting | bytes 16777216 | tf_op jit(solution)/shard_map/reshape | solution.py:571
  1077.5 73.8 %all-reduce.4.cloned.1.call-done = bf16[512,2048]{0,1:T(8,128)(2,1)} async-done(((bf16[512,2048]{0,1:T(8,128)(2,1)}), bf16[512,2048]{0,1:T(8,128)(2,1)}) %all-reduce.4.cloned.1.call-update) | async-done | bytes 2097168 | tf_op jit(solution)/shard_map/psum | solution.py:558
  (509 shorter events, 294.6 us)
Async XLA Ops:
  7.2 39.6 %all-gather.9.cloned.1.call-start = ((), (), s32[]{:S(2)}) async-start(), calls=%async_computation.3 | async-start | bytes 5242880 | tf_op jit(solution)/shard_map/all_gather | solution.py:356
  7.9 178.8 %all-gather.11.cloned.1.call-start = ((), (), s32[]{:S(2)}) async-start(), calls=%async_computation.8 | async-start | bytes 9437184 | tf_op jit(solution)/shard_map/all_gather | solution.py:364
  62.1 198.3 %all-gather.13.cloned.1.call-start = ((), (), s32[]{:S(2)}) async-start(), calls=%async_computation.9 | async-start | bytes 4718592 | tf_op jit(solution)/shard_map/all_gather | solution.py:401
  134.8 25.6 %collective-permute-start.4 = (bf16[1024,512]{1,0:T(8,128)(2,1)}, bf16[1024,512]{1,0:T(8,128)(2,1)}, u32[]{:S(2)}, u32[]{:S(2)}) collective-permute-start(bf16[1024,512]{1,0:T(8,128)(2,1)} %add_convert_fusion.8), channel_id=1, source_target_pairs={{0,2},{1,3},{2,0},{3,1},{4,6},{5,7},{6,4},{7,5},{8,10},{9,11},{10,... | collective-permute-start | bytes 3145736 | tf_op jit(solution)/shard_map/ppermute | solution.py:280
  189.0 209.3 %all-gather.15.cloned.1.call-start = ((), (), s32[]{:S(2)}) async-start(), calls=%async_computation.10 | async-start | bytes 4718592 | tf_op jit(solution)/shard_map/all_gather | solution.py:401
  189.0 140.4 %collective-permute-start.10 = (bf16[8,2,512,512]{3,2,1,0:T(8,128)(2,1)}, bf16[8,2,512,512]{3,2,1,0:T(8,128)(2,1)}, u32[]{:S(2)}, u32[]{:S(2)}) collective-permute-start(bf16[8,2,512,512]{3,2,1,0:T(8,128)(2,1)} %bitcast.309), channel_id=1, source_target_pairs={{0,1},{1,0},{2,3},{3,2},{4,5},{5,4},{6,7},{7,6},{8,9},{9,8},{10,11... | collective-permute-start | bytes 25165832 | tf_op jit(solution)/shard_map/ppermute | solution.py:277
  189.1 140.3 %collective-permute-start.11 = (bf16[2048,1024]{1,0:T(8,128)(2,1)}, bf16[2048,1024]{1,0:T(8,128)(2,1)}, u32[]{:S(2)}, u32[]{:S(2)}) collective-permute-start(bf16[2048,1024]{1,0:T(8,128)(2,1)} %pad_maximum_fusion.2.gate_up_own), channel_id=1, source_target_pairs={{0,2},{1,3},{2,0},{3,1},{4,6},{5,7},{6,4},{7,5},{8,10},{9,11},{10,... | collective-permute-start | bytes 12582920 | tf_op jit(solution)/shard_map/ppermute | solution.py:280
  260.4 69.0 %collective-permute-start.9 = (bf16[8,2,256,512]{3,2,1,0:T(8,128)(2,1)}, bf16[8,2,256,512]{3,2,1,0:T(8,128)(2,1)}, u32[]{:S(2)}, u32[]{:S(2)}) collective-permute-start(bf16[8,2,256,512]{3,2,1,0:T(8,128)(2,1)} %bitcast.329), channel_id=1, source_target_pairs={{0,1},{1,0},{2,3},{3,2},{4,5},{5,4},{6,7},{7,6},{8,9},{9,8},{10,11... | collective-permute-start | bytes 12582920 | tf_op jit(solution)/shard_map/ppermute | solution.py:277
  260.4 310.5 %reduce-scatter.4.cloned.1.call-start = ((), (), s32[]{:S(2)}) async-start(), calls=%async_computation.4 | async-start | bytes 5013504 | tf_op jit(solution)/shard_map/reduce_scatter | solution.py:310
  267.9 17.0 %collective-permute-start.6 = (f32[17,1024]{1,0:T(8,128)S(1)}, f32[17,1024]{1,0:T(8,128)S(1)}, u32[]{:S(2)}, u32[]{:S(2)}) collective-permute-start(f32[17,1024]{1,0:T(8,128)S(1)} %fusion.115), channel_id=1, source_target_pairs={{0,2},{1,3},{2,0},{3,1},{4,6},{5,7},{6,4},{7,5},{8,10},{9,11},{10,... | collective-permute-start | bytes 208904 | tf_op jit(solution)/shard_map/ppermute | solution.py:280
  269.5 60.0 %collective-permute-start.12 = (bf16[512,2048]{1,0:T(8,128)(2,1)}, bf16[512,2048]{1,0:T(8,128)(2,1)}, u32[]{:S(2)}, u32[]{:S(2)}) collective-permute-start(bf16[512,2048]{1,0:T(8,128)(2,1)} %bitcast.22.down_own), channel_id=1, source_target_pairs={{0,2},{1,3},{2,0},{3,1},{4,6},{5,7},{6,4},{7,5},{8,10},{9,11},{10,... | collective-permute-start | bytes 6291464 | tf_op jit(solution)/shard_map/ppermute | solution.py:280
  398.3 14.8 %collective-permute-start.14 = (bf16[8,2,256,512]{3,2,1,0:T(8,128)(2,1)}, bf16[8,2,256,512]{3,2,1,0:T(8,128)(2,1)}, u32[]{:S(2)}, u32[]{:S(2)}) collective-permute-start(bf16[8,2,256,512]{3,2,1,0:T(8,128)(2,1)} %bitcast.340), channel_id=1, source_target_pairs={{0,1},{1,0},{2,3},{3,2},{4,5},{5,4},{6,7},{7,6},{8,9},{9,8},{10,11... | collective-permute-start | bytes 12582920 | tf_op jit(solution)/shard_map/ppermute | solution.py:277
  412.9 185.5 %reduce-scatter.6.cloned.1.call-start = ((), (), s32[]{:S(2)}) async-start(), calls=%async_computation.5 | async-start | bytes 5013504 | tf_op jit(solution)/shard_map/reduce_scatter | solution.py:310
  464.3 28.6 %collective-permute-start.15 = (bf16[8,2,256,512]{3,2,1,0:T(8,128)(2,1)}, bf16[8,2,256,512]{3,2,1,0:T(8,128)(2,1)}, u32[]{:S(2)}, u32[]{:S(2)}) collective-permute-start(bf16[8,2,256,512]{3,2,1,0:T(8,128)(2,1)} %get-tuple-element.71), channel_id=1, source_target_pairs={{0,1},{1,0},{2,3},{3,2},{4,5},{5,4},{6,7},{7,6},{8,9},{9,8},{10,11... | collective-permute-start | bytes 12582920 | tf_op jit(solution)/shard_map/ppermute | solution.py:277
  464.5 86.1 %collective-permute-start.16 = (bf16[8,2,256,512]{3,2,1,0:T(8,128)(2,1)}, bf16[8,2,256,512]{3,2,1,0:T(8,128)(2,1)}, u32[]{:S(2)}, u32[]{:S(2)}) collective-permute-start(bf16[8,2,256,512]{3,2,1,0:T(8,128)(2,1)} %get-tuple-element.74), channel_id=1, source_target_pairs={{0,1},{1,0},{2,3},{3,2},{4,5},{5,4},{6,7},{7,6},{8,9},{9,8},{10,11... | collective-permute-start | bytes 12582920 | tf_op jit(solution)/shard_map/ppermute | solution.py:277
  468.7 89.0 %collective-permute-start.17 = (bf16[8,2,256,512]{3,2,1,0:T(8,128)(2,1)}, bf16[8,2,256,512]{3,2,1,0:T(8,128)(2,1)}, u32[]{:S(2)}, u32[]{:S(2)}) collective-permute-start(bf16[8,2,256,512]{3,2,1,0:T(8,128)(2,1)} %get-tuple-element.76), channel_id=1, source_target_pairs={{0,1},{1,0},{2,3},{3,2},{4,5},{5,4},{6,7},{7,6},{8,9},{9,8},{10,11... | collective-permute-start | bytes 12582920 | tf_op jit(solution)/shard_map/ppermute | solution.py:277
  498.9 552.7 %reduce-scatter.8.cloned.1.call-start = ((), (), s32[]{:S(2)}) async-start(), calls=%async_computation.6 | async-start | bytes 9437184 | tf_op jit(solution)/shard_map/reduce_scatter | solution.py:310
  603.9 14.3 %collective-permute-start.18 = (bf16[512,512]{1,0:T(8,128)(2,1)}, bf16[512,512]{1,0:T(8,128)(2,1)}, u32[]{:S(2)}, u32[]{:S(2)}) collective-permute-start(bf16[512,512]{1,0:T(8,128)(2,1)} %slice_bitcast_fusion.8), channel_id=1, source_target_pairs={{0,2},{1,3},{2,0},{3,1},{4,6},{5,7},{6,4},{7,5},{8,10},{9,11},{10,... | collective-permute-start | bytes 1572872 | tf_op jit(solution)/shard_map/ppermute | solution.py:280
  633.0 24.4 %collective-permute-start.24 = (bf16[1024,512]{1,0:T(8,128)(2,1)}, bf16[1024,512]{1,0:T(8,128)(2,1)}, u32[]{:S(2)}, u32[]{:S(2)}) collective-permute-start(bf16[1024,512]{1,0:T(8,128)(2,1)} %fusion.119), channel_id=1, source_target_pairs={{0,2},{1,3},{2,0},{3,1},{4,6},{5,7},{6,4},{7,5},{8,10},{9,11},{10,... | collective-permute-start | bytes 3145736 | tf_op jit(solution)/shard_map/ppermute | solution.py:280
  634.2 517.1 %all-reduce.4.cloned.1.call-start = ((), (), s32[]{:S(2)}) async-start(), calls=%async_computation.7 | async-start | bytes 4194304 | tf_op jit(solution)/shard_map/psum | solution.py:558
  634.2 25.9 %collective-permute-start.23 = (bf16[1024,512]{1,0:T(8,128)(2,1)}, bf16[1024,512]{1,0:T(8,128)(2,1)S(1)}, u32[]{:S(2)}, u32[]{:S(2)}) collective-permute-start(bf16[1024,512]{1,0:T(8,128)(2,1)} %fusion.119), channel_id=1, source_target_pairs={{0,1},{1,0},{2,3},{3,2},{4,5},{5,4},{6,7},{7,6},{8,9},{9,8},{10,11... | collective-permute-start | bytes 3145736 | tf_op jit(solution)/shard_map/ppermute | solution.py:277
  698.6 75.4 %collective-permute-start.61 = (bf16[4,256,512]{2,1,0:T(8,128)(2,1)}, bf16[4,256,512]{2,1,0:T(8,128)(2,1)}, u32[]{:S(2)}, u32[]{:S(2)}) collective-permute-start(bf16[4,256,512]{2,1,0:T(8,128)(2,1)} %dynamic-slice_bitcast_fusion), channel_id=1, source_target_pairs={{0,4},{4,0},{8,12},{12,8},{16,20},{20,16},{24,28},{28,24},{1,5},{5... | collective-permute-start | bytes 3145736 | tf_op jit(solution)/shard_map/ppermute | solution.py:283
  700.1 332.8 %collective-permute-start.73 = (bf16[512,2048]{1,0:T(8,128)(2,1)}, bf16[512,2048]{1,0:T(8,128)(2,1)}, u32[]{:S(2)}, u32[]{:S(2)}) collective-permute-start(bf16[512,2048]{1,0:T(8,128)(2,1)} %bitcast_convert_fusion.1), channel_id=1, source_target_pairs={{0,2},{1,3},{2,0},{3,1},{4,6},{5,7},{6,4},{7,5},{8,10},{9,11},{10,... | collective-permute-start | bytes 6291464 | tf_op jit(solution)/shard_map/ppermute | solution.py:280
  710.4 38.0 %collective-permute-start.28 = (f32[2,1024]{1,0:T(2,128)S(1)}, f32[2,1024]{1,0:T(2,128)S(1)}, u32[]{:S(2)}, u32[]{:S(2)}) collective-permute-start(f32[2,1024]{1,0:T(2,128)S(1)} %fusion.116), channel_id=1, source_target_pairs={{0,2},{1,3},{2,0},{3,1},{4,6},{5,7},{6,4},{7,5},{8,10},{9,11},{10,... | collective-permute-start | bytes 24584 | tf_op jit(solution)/shard_map/ppermute | solution.py:280
  759.9 33.2 %collective-permute-start.50 = (bf16[4,256,512]{2,1,0:T(8,128)(2,1)S(1)}, bf16[4,256,512]{2,1,0:T(8,128)(2,1)S(1)}, u32[]{:S(2)}, u32[]{:S(2)}) collective-permute-start(bf16[4,256,512]{2,1,0:T(8,128)(2,1)S(1)} %dynamic-slice_bitcast_fusion.1), channel_id=1, source_target_pairs={{0,4},{4,0},{8,12},{12,8},{16,20},{20,16},{24,28},{28,24},{1,5},{5... | collective-permute-start | bytes 3145736 | tf_op jit(solution)/shard_map/ppermute | solution.py:283
  769.1 46.1 %collective-permute-start.39 = (bf16[4,256,512]{2,1,0:T(8,128)(2,1)S(1)}, bf16[4,256,512]{2,1,0:T(8,128)(2,1)S(1)}, u32[]{:S(2)}, u32[]{:S(2)}) collective-permute-start(bf16[4,256,512]{2,1,0:T(8,128)(2,1)S(1)} %dynamic-slice_bitcast_fusion.2), channel_id=1, source_target_pairs={{0,4},{4,0},{8,12},{12,8},{16,20},{20,16},{24,28},{28,24},{1,5},{5... | collective-permute-start | bytes 3145736 | tf_op jit(solution)/shard_map/ppermute | solution.py:283
  774.1 43.1 %collective-permute-start.30 = (bf16[1024,512]{1,0:T(8,128)(2,1)S(1)}, bf16[1024,512]{1,0:T(8,128)(2,1)S(1)}, u32[]{:S(2)}, u32[]{:S(2)}) collective-permute-start(bf16[1024,512]{1,0:T(8,128)(2,1)S(1)} %add_convert_fusion.5), channel_id=1, source_target_pairs={{0,1},{1,0},{2,3},{3,2},{4,5},{5,4},{6,7},{7,6},{8,9},{9,8},{10,11... | collective-permute-start | bytes 3145736 | tf_op jit(solution)/shard_map/ppermute | solution.py:277
  774.1 71.2 %collective-permute-start.29 = (bf16[1024,512]{1,0:T(8,128)(2,1)S(1)}, bf16[1024,512]{1,0:T(8,128)(2,1)S(1)}, u32[]{:S(2)}, u32[]{:S(2)}) collective-permute-start(bf16[1024,512]{1,0:T(8,128)(2,1)S(1)} %add_convert_fusion.6), channel_id=1, source_target_pairs={{0,1},{1,0},{2,3},{3,2},{4,5},{5,4},{6,7},{7,6},{8,9},{9,8},{10,11... | collective-permute-start | bytes 3145736 | tf_op jit(solution)/shard_map/ppermute | solution.py:277
  793.1 26.7 %collective-permute-start.62 = (bf16[256,512]{1,0:T(8,128)(2,1)S(1)}, bf16[256,512]{1,0:T(8,128)(2,1)S(1)}, u32[]{:S(2)}, u32[]{:S(2)}) collective-permute-start(bf16[256,512]{1,0:T(8,128)(2,1)S(1)} %fusion.76), channel_id=1, source_target_pairs={{0,8},{4,12},{8,16},{12,20},{16,24},{20,28},{24,0},{28,4},{1,9},{5... | collective-permute-start | bytes 786440 | tf_op jit(solution)/shard_map/ppermute | solution.py:286
  815.3 15.5 %collective-permute-start.51 = (bf16[256,512]{1,0:T(8,128)(2,1)S(1)}, bf16[256,512]{1,0:T(8,128)(2,1)S(1)}, u32[]{:S(2)}, u32[]{:S(2)}) collective-permute-start(bf16[256,512]{1,0:T(8,128)(2,1)S(1)} %fusion.75), channel_id=1, source_target_pairs={{0,8},{4,12},{8,16},{12,20},{16,24},{20,28},{24,0},{28,4},{1,9},{5... | collective-permute-start | bytes 786440 | tf_op jit(solution)/shard_map/ppermute | solution.py:286
  819.9 26.1 %collective-permute-start.31 = (bf16[1024,512]{1,0:T(8,128)(2,1)S(1)}, bf16[1024,512]{1,0:T(8,128)(2,1)S(1)}, u32[]{:S(2)}, u32[]{:S(2)}) collective-permute-start(bf16[1024,512]{1,0:T(8,128)(2,1)S(1)} %add_convert_fusion.4), channel_id=1, source_target_pairs={{0,2},{1,3},{2,0},{3,1},{4,6},{5,7},{6,4},{7,5},{8,10},{9,11},{10,... | collective-permute-start | bytes 3145736 | tf_op jit(solution)/shard_map/ppermute | solution.py:280
  830.8 14.5 %collective-permute-start.41 = (bf16[256,512]{1,0:T(8,128)(2,1)S(1)}, bf16[256,512]{1,0:T(8,128)(2,1)S(1)}, u32[]{:S(2)}, u32[]{:S(2)}) collective-permute-start(bf16[256,512]{1,0:T(8,128)(2,1)S(1)} %fusion.30), channel_id=1, source_target_pairs={{0,8},{4,12},{8,16},{12,20},{16,24},{20,28},{24,0},{28,4},{1,9},{5... | collective-permute-start | bytes 786440 | tf_op jit(solution)/shard_map/ppermute | solution.py:286
  841.7 191.3 %collective-permute-start.72 = (bf16[2048,1024]{1,0:T(8,128)(2,1)}, bf16[2048,1024]{1,0:T(8,128)(2,1)}, u32[]{:S(2)}, u32[]{:S(2)}) collective-permute-start(bf16[2048,1024]{1,0:T(8,128)(2,1)} %bitcast_convert_fusion), channel_id=1, source_target_pairs={{0,2},{1,3},{2,0},{3,1},{4,6},{5,7},{6,4},{7,5},{8,10},{9,11},{10,... | collective-permute-start | bytes 12582920 | tf_op jit(solution)/shard_map/ppermute | solution.py:280
  845.3 16.9 %collective-permute-start.64 = (bf16[256,512]{1,0:T(8,128)(2,1)}, bf16[256,512]{1,0:T(8,128)(2,1)}, u32[]{:S(2)}, u32[]{:S(2)}) collective-permute-start(bf16[256,512]{1,0:T(8,128)(2,1)} %fusion.25), channel_id=1, source_target_pairs={{0,8},{4,12},{8,16},{12,20},{16,24},{20,28},{24,0},{28,4},{1,9},{5... | collective-permute-start | bytes 786440 | tf_op jit(solution)/shard_map/ppermute | solution.py:286
  846.0 25.5 %collective-permute-start.42 = (bf16[256,512]{1,0:T(8,128)(2,1)S(1)}, bf16[256,512]{1,0:T(8,128)(2,1)}, u32[]{:S(2)}, u32[]{:S(2)}) collective-permute-start(bf16[256,512]{1,0:T(8,128)(2,1)S(1)} %fusion.31), channel_id=1, source_target_pairs={{0,8},{4,12},{8,16},{12,20},{16,24},{20,28},{24,0},{28,4},{1,9},{5... | collective-permute-start | bytes 786440 | tf_op jit(solution)/shard_map/ppermute | solution.py:286
  860.6 25.4 %collective-permute-start.53 = (bf16[256,512]{1,0:T(8,128)(2,1)S(1)}, bf16[256,512]{1,0:T(8,128)(2,1)S(1)}, u32[]{:S(2)}, u32[]{:S(2)}) collective-permute-start(bf16[256,512]{1,0:T(8,128)(2,1)S(1)} %fusion.28), channel_id=1, source_target_pairs={{0,8},{4,12},{8,16},{12,20},{16,24},{20,28},{24,0},{28,4},{1,9},{5... | collective-permute-start | bytes 786440 | tf_op jit(solution)/shard_map/ppermute | solution.py:286
  871.5 15.8 %collective-permute-start.65 = (bf16[256,512]{1,0:T(8,128)(2,1)S(1)}, bf16[256,512]{1,0:T(8,128)(2,1)S(1)}, u32[]{:S(2)}, u32[]{:S(2)}) collective-permute-start(bf16[256,512]{1,0:T(8,128)(2,1)S(1)} %fusion.26), channel_id=1, source_target_pairs={{0,8},{4,12},{8,16},{12,20},{16,24},{20,28},{24,0},{28,4},{1,9},{5... | collective-permute-start | bytes 786440 | tf_op jit(solution)/shard_map/ppermute | solution.py:286
  871.5 14.5 %collective-permute-start.36 = (f32[20,512]{1,0:T(8,128)S(1)}, f32[20,512]{1,0:T(8,128)S(1)}, u32[]{:S(2)}, u32[]{:S(2)}) collective-permute-start(f32[20,512]{1,0:T(8,128)S(1)} %add.435), channel_id=1, source_target_pairs={{0,16},{4,20},{8,24},{12,28},{16,0},{20,4},{24,8},{28,12},{1,17},{... | collective-permute-start | bytes 122888 | tf_op jit(solution)/shard_map/ppermute | solution.py:580
  887.3 14.2 %collective-permute-start.66 = (bf16[256,512]{1,0:T(8,128)(2,1)S(1)}, bf16[256,512]{1,0:T(8,128)(2,1)S(1)}, u32[]{:S(2)}, u32[]{:S(2)}) collective-permute-start(bf16[256,512]{1,0:T(8,128)(2,1)S(1)} %collective-permute-done.65), channel_id=1, source_target_pairs={{0,8},{4,12},{8,16},{12,20},{16,24},{20,28},{24,0},{28,4},{1,9},{5... | collective-permute-start | bytes 786440 | tf_op jit(solution)/shard_map/ppermute | solution.py:286
  887.6 50.8 %collective-permute-start.38 = (f32[18,2048]{1,0:T(8,128)S(1)}, f32[18,2048]{1,0:T(8,128)S(1)}, u32[]{:S(2)}, u32[]{:S(2)}) collective-permute-start(f32[18,2048]{1,0:T(8,128)S(1)} %add_dynamic-update-slice_fusion), channel_id=1, source_target_pairs={{0,2},{1,3},{2,0},{3,1},{4,6},{5,7},{6,4},{7,5},{8,10},{9,11},{10,... | collective-permute-start | bytes 442376 | tf_op jit(solution)/shard_map/ppermute | solution.py:280
  895.8 45.3 %collective-permute-start.54 = (bf16[256,512]{1,0:T(8,128)(2,1)S(1)}, bf16[256,512]{1,0:T(8,128)(2,1)S(1)}, u32[]{:S(2)}, u32[]{:S(2)}) collective-permute-start(bf16[256,512]{1,0:T(8,128)(2,1)S(1)} %fusion.29), channel_id=1, source_target_pairs={{0,8},{4,12},{8,16},{12,20},{16,24},{20,28},{24,0},{28,4},{1,9},{5... | collective-permute-start | bytes 786440 | tf_op jit(solution)/shard_map/ppermute | solution.py:286
  901.4 40.2 %collective-permute-start.44 = (bf16[256,512]{1,0:T(8,128)(2,1)S(1)}, bf16[256,512]{1,0:T(8,128)(2,1)S(1)}, u32[]{:S(2)}, u32[]{:S(2)}) collective-permute-start(bf16[256,512]{1,0:T(8,128)(2,1)S(1)} %collective-permute-done.43), channel_id=1, source_target_pairs={{0,8},{4,12},{8,16},{12,20},{16,24},{20,28},{24,0},{28,4},{1,9},{5... | collective-permute-start | bytes 786440 | tf_op jit(solution)/shard_map/ppermute | solution.py:286
  941.1 35.7 %collective-permute-start.70 = (bf16[256,512]{1,0:T(8,128)(2,1)S(1)}, bf16[256,512]{1,0:T(8,128)(2,1)S(1)}, u32[]{:S(2)}, u32[]{:S(2)}) collective-permute-start(bf16[256,512]{1,0:T(8,128)(2,1)S(1)} %collective-permute-done.65), channel_id=1, source_target_pairs={{0,4},{4,0},{8,12},{12,8},{16,20},{20,16},{24,28},{28,24},{1,5},{5... | collective-permute-start | bytes 786440 | tf_op jit(solution)/shard_map/ppermute | solution.py:283
  954.9 19.8 %collective-permute-start.69 = (bf16[256,512]{1,0:T(8,128)(2,1)S(1)}, bf16[256,512]{1,0:T(8,128)(2,1)S(1)}, u32[]{:S(2)}, u32[]{:S(2)}) collective-permute-start(bf16[256,512]{1,0:T(8,128)(2,1)S(1)} %collective-permute-done.66), channel_id=1, source_target_pairs={{0,4},{4,0},{8,12},{12,8},{16,20},{20,16},{24,28},{28,24},{1,5},{5... | collective-permute-start | bytes 786440 | tf_op jit(solution)/shard_map/ppermute | solution.py:283
  974.7 25.4 %collective-permute-start.48 = (bf16[256,512]{1,0:T(8,128)(2,1)S(1)}, bf16[256,512]{1,0:T(8,128)(2,1)S(1)}, u32[]{:S(2)}, u32[]{:S(2)}) collective-permute-start(bf16[256,512]{1,0:T(8,128)(2,1)S(1)} %collective-permute-done.43), channel_id=1, source_target_pairs={{0,4},{4,0},{8,12},{12,8},{16,20},{20,16},{24,28},{28,24},{1,5},{5... | collective-permute-start | bytes 786440 | tf_op jit(solution)/shard_map/ppermute | solution.py:283
  976.8 21.2 %collective-permute-start.47 = (bf16[256,512]{1,0:T(8,128)(2,1)S(1)}, bf16[256,512]{1,0:T(8,128)(2,1)S(1)}, u32[]{:S(2)}, u32[]{:S(2)}) collective-permute-start(bf16[256,512]{1,0:T(8,128)(2,1)S(1)} %collective-permute-done.44), channel_id=1, source_target_pairs={{0,4},{4,0},{8,12},{12,8},{16,20},{20,16},{24,28},{28,24},{1,5},{5... | collective-permute-start | bytes 786440 | tf_op jit(solution)/shard_map/ppermute | solution.py:283
  998.0 22.9 %collective-permute-start.59 = (bf16[256,512]{1,0:T(8,128)(2,1)S(1)}, bf16[256,512]{1,0:T(8,128)(2,1)S(1)}, u32[]{:S(2)}, u32[]{:S(2)}) collective-permute-start(bf16[256,512]{1,0:T(8,128)(2,1)S(1)} %collective-permute-done.54), channel_id=1, source_target_pairs={{0,4},{4,0},{8,12},{12,8},{16,20},{20,16},{24,28},{28,24},{1,5},{5... | collective-permute-start | bytes 786440 | tf_op jit(solution)/shard_map/ppermute | solution.py:283
  1000.2 20.7 %collective-permute-start.58 = (bf16[256,512]{1,0:T(8,128)(2,1)S(1)}, bf16[256,512]{1,0:T(8,128)(2,1)S(1)}, u32[]{:S(2)}, u32[]{:S(2)}) collective-permute-start(bf16[256,512]{1,0:T(8,128)(2,1)S(1)} %collective-permute-done.55), channel_id=1, source_target_pairs={{0,4},{4,0},{8,12},{12,8},{16,20},{20,16},{24,28},{28,24},{1,5},{5... | collective-permute-start | bytes 786440 | tf_op jit(solution)/shard_map/ppermute | solution.py:283
  (101 other events, 1112.5 us)
Sparse Core Ops, SparseCore 0:
  9.6 37.1 all-gather.8
  62.2 124.4 all-gather.10
  189.4 70.9 all-gather.12
  262.4 80.4 all-gather.14
  413.0 90.1 reduce-scatter.3
  506.6 91.7 reduce-scatter.5
  634.3 161.4 reduce-scatter.7
  1051.7 99.5 all-reduce.3
where the time goes:
time: 1180 us; the launch traced here: 1170 us
  waiting for transfers between devices  573 us (49%)
  Pallas kernels  147 us (12%)
  matrix products  140 us (12%)
  other arithmetic  126 us (11%)
  local copies, waits for them, and re-layouts  83.7 us (7%)
  starting transfers between devices  46.5 us (4%)
  blocking collectives  34.9 us (3%)
  between operations  17 us (1%)
    ppermute x18, waiting for transfers between devices, over_x(): return lax.ppermute(v, 'tensor', [(i, i ^ 2) for i in range(n_tensor)])  175 us
    pallas_call x2, Pallas kernels, act_call(): pl.pallas_call(functools.partial(act_body, n_local, len(before)), out_sha...  120 us
    dot_general x12, matrix products, cross_dot(): lax.dot_general(operand, other_side, (((0,), (0,)), ((), ())), preferred_...  94.2 us
    ppermute x15, waiting for transfers between devices, over_y(): return lax.ppermute(v, 'expert', [(i, i ^ 1) for i in range(n_expert)])  88.4 us
    psum x1, waiting for transfers between devices, layer(): sum_out = lax.psum(ready, 'expert').astype(f32)  73.8 us
    all_gather x2, waiting for transfers between devices, layer(): lax.all_gather(v, 'expert', axis=0)  69.8 us
    ppermute x18, waiting for transfers between devices, over_z(): lax.ppermute(v, 'expert', [(i, (i + 2) % n_expert) for i in range(n_exper...  63.6 us
    all_gather x1, blocking collectives, layer(): flat = lax.all_gather(flat, 'expert', axis=0)  34.9 us
  transfers between devices with their start and end apart: 82, of which 47 were waited for; matrix products, arithmetic and copies ran while one was open for 27% of the time, Pallas kernels for 13%

commit v1 on v0

--- a/solution.py
+++ b/solution.py
@@ -390,7 +390,7 @@
             heads_out,
             lax.dynamic_slice_in_dim(w_out, at, slice_width, 1),
             preferred_element_type=f32,
-        )
+        ),
     )
     hidden = block_input.astype(f32) + attn_slice
     g_moe_slice = own_columns(g_moe)
@@ -425,6 +425,7 @@
         axis=0,
     )
     flat = lax.all_gather(flat, "expert", axis=0)
+    x_near[0], flat = lax.optimization_barrier((x_near[0], flat))
     all_lengths = flat[:, n_experts + 1, 0].astype(jnp.int32)
     info = jnp.concatenate(
         [
@@ -466,14 +467,14 @@
     x_stack, g_stack, pre_own, pre_other, inner_own, inner_other = [
         v.reshape(-1, v.shape[3]) for v in stacks
     ]
+    other_down = over_x(cross_dot(inner_other, g_stack).astype(bf16))
     other_gu = cross_dot(x_stack, pre_other).astype(bf16)
-    other_down = cross_dot(inner_other, g_stack).astype(bf16)
     mine_gu = cross_dot(x_stack, pre_own)
     mine_down = cross_dot(inner_own, g_stack)
     out_message = jnp.concatenate([joined(parts) for parts in out_parts], axis=2)
     back_total = jnp.concatenate(back_parts, axis=1)
-    back_total, out_message, other_gu, other_down, mine_gu, mine_down = lax.optimization_barrier(
-        (back_total, out_message, other_gu, other_down, mine_gu, mine_down)
+    back_total, out_message, other_gu, mine_gu, mine_down = lax.optimization_barrier(
+        (back_total, out_message, other_gu, mine_gu, mine_down)
     )
     back_slice = home(back_total)
     moe_total = reduced(out_message)
@@ -505,8 +506,7 @@
         for p, v in enumerate(d_attn)
     )
     d_heads = d_heads.astype(bf16)
-    other_gu, other_down, _ = lax.optimization_barrier((other_gu, other_down, d_attn[3]))
-    other_gu, other_down = over_x(other_gu), over_x(other_down)
+    other_gu = over_x(other_gu)
     d_query, d_keys, d_values = per_head(
         attend_back_body,
         lengths,
@@ -554,8 +554,8 @@
     ).astype(jnp.bfloat16)
 
     sum_query, sum_key, sum_value = map(expert_sum, (grad_w_query, grad_w_key, grad_w_value))
-    ready, moe_total = lax.optimization_barrier((grad_w_out.astype(bf16), moe_total))
-    sum_out = lax.psum(ready, "expert").astype(f32)
+    sum_out = lax.psum(grad_w_out.astype(bf16), "expert")
+    sum_out = sum_out.astype(f32)
     moe_slice = home(moe_total)
     output = (valid_rows * (hidden + moe_slice)).astype(bf16)
     sum_out = jnp.concatenate(

time: 1180 us -> 1160 us (0.983)
  waiting for transfers between devices: 573 us -> 515 us
  starting transfers between devices: 46.5 us -> 67.8 us
    psum x1, waiting for transfers between devices: 73.8 us -> 0.01 us  [layer(): sum_out = lax.psum(grad_w_out.astype(bf16), 'expert')]
    ppermute x18, waiting for transfers between devices: 175 us -> 247 us  [over_x(): return lax.ppermute(v, 'tensor', [(i, i ^ 2) for i in range(n_tensor)])]
    all_gather x2, waiting for transfers between devices: 69.8 us -> 23.1 us  [layer(): lax.all_gather(v, 'expert', axis=0)]
    ppermute x3, waiting for transfers between devices: 23.2 us -> 2.66 us  [layer(): lax.ppermute(small, 'expert', [(i, i ^ hop) for i in range(n_expert)])]
    ppermute x18, starting transfers between devices: 9.49 us -> 27.1 us  [over_z(): lax.ppermute(v, 'expert', [(i, (i + 2) % n_expert) for i in range(n_exper...]
    unnamed x176 -> x164, local copies, waits for them, and re-layouts: 25.6 us -> 28.6 us
  transfers between devices with their start and end apart: 82 -> 82, of which waited for: 47 -> 39; matrix products, arithmetic and copies ran while one was open for 27% -> 30% of each run, Pallas kernels for 13% -> 13%
where the time goes in v1:
time: 1160 us; the launch traced here: 1150 us
  waiting for transfers between devices  515 us (44%)
  Pallas kernels  147 us (13%)
  matrix products  146 us (13%)
  other arithmetic  131 us (11%)
  local copies, waits for them, and re-layouts  91.7 us (8%)
  starting transfers between devices  67.8 us (6%)
  blocking collectives  36.9 us (3%)
  between operations  17.1 us (1%)
    ppermute x18, waiting for transfers between devices, over_x(): return lax.ppermute(v, 'tensor', [(i, i ^ 2) for i in range(n_tensor)])  247 us
    pallas_call x2, Pallas kernels, act_call(): pl.pallas_call(functools.partial(act_body, n_local, len(before)), out_sha...  120 us
    dot_general x12, matrix products, cross_dot(): lax.dot_general(operand, other_side, (((0,), (0,)), ((), ())), preferred_...  95.1 us
    ppermute x15, waiting for transfers between devices, over_y(): return lax.ppermute(v, 'expert', [(i, i ^ 1) for i in range(n_expert)])  86.6 us
    ppermute x18, waiting for transfers between devices, over_z(): lax.ppermute(v, 'expert', [(i, (i + 2) % n_expert) for i in range(n_exper...  55.8 us
    all_gather x1, blocking collectives, layer(): flat = lax.all_gather(flat, 'expert', axis=0)  36.9 us
    reduce_scatter x3, waiting for transfers between devices, reduced(): return lax.psum_scatter(message, 'expert', scatter_dimension=0)  34.3 us
    all_gather x1, waiting for transfers between devices, layer(): full_input = lax.all_gather(block_input, 'tensor', axis=1, tiled=True)  34 us
  transfers between devices with their start and end apart: 82, of which 39 were waited for; matrix products, arithmetic and copies ran while one was open for 30% of the time, Pallas kernels for 13%

profile of v1, /device:TPU:0, one launch (start us, length us, event | category | flops | bytes accessed | tf_op | source)
XLA Modules:
  0.0 1151.9 jit_solution(15331129890148365358)
XLA Ops:
  12.8 34.0 %all-gather.9.cloned.1.call-done = bf16[1024,2048]{1,0:T(8,128)(2,1)} async-done(((bf16[1024,512]{1,0:T(8,128)(2,1)}), bf16[1024,2048]{1,0:T(8,128)(2,1)}) %all-gather.9.cloned.1.call-update) | async-done | bytes 4194320 | tf_op jit(solution)/shard_map/all_gather | solution.py:356
  47.3 13.7 %collective-permute-done.6 = bf16[512,512]{1,0:T(8,128)(2,1)S(1)} collective-permute-done((bf16[512,512]{1,0:T(8,128)(2,1)S(1)}, bf16[512,512]{1,0:T(8,128)(2,1)S(1)}, u32[]{:S(2)}, u32[]{:S(2)}) %collective-permute-start.6) | collective-permute-done | bytes 524320 | tf_op jit(solution)/shard_map/ppermute | solution.py:280
  65.6 5.7 multiply_reduce_fusion.3
  78.4 6.3 convolution_convert_fusion.5.v_ref
  102.8 6.3 subtract_convert_fusion
  114.3 10.9 shard_map.263
  137.4 22.4 %collective-permute-done.4 = bf16[1024,512]{1,0:T(8,128)(2,1)} collective-permute-done((bf16[1024,512]{1,0:T(8,128)(2,1)}, bf16[1024,512]{1,0:T(8,128)(2,1)}, u32[]{:S(2)}, u32[]{:S(2)}) %collective-permute-start.4) | collective-permute-done | bytes 1048608 | tf_op jit(solution)/shard_map/ppermute | solution.py:280
  164.9 11.4 collective-permute-done.5
  177.4 9.3 all-gather.11.cloned.1.call-done
  191.0 11.6 %collective-permute-done.7 = f32[17,1024]{1,0:T(8,128)S(1)} collective-permute-done((f32[17,1024]{1,0:T(8,128)S(1)}, f32[17,1024]{1,0:T(8,128)S(1)}, u32[]{:S(2)}, u32[]{:S(2)}) %collective-permute-start.7) | collective-permute-done | bytes 69664 | tf_op jit(solution)/shard_map/ppermute | solution.py:277
  208.4 36.9 %all-gather.2 = f32[192,1024]{1,0:T(8,128)} all-gather(f32[24,1024]{1,0:T(8,128)S(1)} %maximum_maximum_fusion.2), channel_id=4, replica_groups=mesh['expert'=8,'tensor'=4] {'expert'}, dimensions={0}, use_global_device_ids=true | all-gather | bytes 884736 | tf_op jit(solution)/shard_map/all_gather | solution.py:427
  245.4 23.1 %all-gather.13.cloned.1.call-done = bf16[16,256,512]{2,1,0:T(8,128)(2,1)} async-done(((bf16[2,256,512]{2,1,0:T(8,128)(2,1)}), bf16[16,256,512]{2,1,0:T(8,128)(2,1)}) %all-gather.13.cloned.1.call-update) | async-done | bytes 4194320 | tf_op jit(solution)/shard_map/all_gather | solution.py:401
  279.5 63.0 %collective-permute-done.12.down_other = bf16[512,2048]{1,0:T(8,128)(2,1)} collective-permute-done((bf16[512,2048]{1,0:T(8,128)(2,1)}, bf16[512,2048]{1,0:T(8,128)(2,1)}, u32[]{:S(2)}, u32[]{:S(2)}) %collective-permute-start.12) | collective-permute-done | bytes 2097184 | tf_op jit(solution)/shard_map/ppermute | solution.py:280
  342.4 68.6 %experts.2 = (bf16[8,2,256,512]{3,2,1,0:T(8,128)(2,1)}, bf16[8,2,256,512]{3,2,1,0:T(8,128)(2,1)}, bf16[8,2,256,512]{3,2,1,0:T(8,128)(2,1)}, bf16[8,2,256,512]{3,...) custom-call(s32[10]{0:T(128)} %get-tuple-element.245.meta, ...), custom_call_target="tpu_custom_call" | custom-call | tf_op jit(solution)/shard_map/experts/pallas_call | solution.py:224
  413.2 5.4 collective-permute-done.13
  418.6 4.8 add_convert_fusion.3
  426.2 51.2 %experts.3 = (bf16[8,2,256,512]{3,2,1,0:T(8,128)(2,1)}, bf16[8,2,256,512]{3,2,1,0:T(8,128)(2,1)}, bf16[8,2,256,512]{3,2,1,0:T(8,128)(2,1)}, bf16[8,2,256,512]{3,...) custom-call(s32[10]{0:T(128)} %get-tuple-element.246.meta, ...), custom_call_target="tpu_custom_call", output_to_operand_aliasing={{4}: (10, {}), {5}: (11, {}), {6}: (12, {}), {7}: (13, {}),... | custom-call | tf_op jit(solution)/shard_map/experts/pallas_call | solution.py:224
  484.9 4.9 add_convert_fusion.2
  492.4 24.3 %bitcast_convert_fusion = bf16[2048,1024]{1,0:T(8,128)(2,1)} fusion(bf16[2,8,256,2048]{3,2,1,0:T(8,128)(2,1)} %get-tuple-element.76, bf16[2,8,256,1024]{3,2,1,0:T(8,128)(2,1)} %get-tuple-element.77), kind=kOutput, calls=%fused_computation.6 | convolution fusion | flops 17181966336 | bytes 29360128 | tf_op jit(solution)/shard_map/dot_general | solution.py:21
  516.7 14.2 %convolution_bitcast_fusion.1 = f32[512,2048]{1,0:T(8,128)} fusion(bf16[2,8,256,512]{3,2,1,0:T(8,128)(2,1)S(1)} %copy-done.35, bf16[2,8,256,2048]{3,2,1,0:T(8,128)(2,1)} %get-tuple-element.80), kind=kOutput, calls=%fused_computation.21 | convolution fusion | flops 8589934592 | bytes 25165824 | tf_op jit(solution)/shard_map/dot_general | solution.py:21
  530.9 24.5 %convolution_bitcast_fusion = f32[2048,1024]{1,0:T(8,128)} fusion(bf16[2,8,256,2048]{3,2,1,0:T(8,128)(2,1)S(1)} %bitcast.320, bf16[2,8,256,1024]{3,2,1,0:T(8,128)(2,1)} %get-tuple-element.78), kind=kOutput, calls=%fused_computation.14 | convolution fusion | flops 17179869184 | bytes 33554432 | tf_op jit(solution)/shard_map/dot_general | solution.py:21
  555.5 5.8 add_convert_fusion.1
  561.3 5.7 add_convert_fusion
  566.9 7.6 pad_maximum_fusion
  577.1 34.3 %reduce-scatter.6.cloned.1.call-done = bf16[1,2,272,512]{3,2,1,0:T(8,128)(2,1)} async-done(((bf16[8,2,272,512]{3,2,1,0:T(8,128)(2,1)}), bf16[1,2,272,512]{3,2,1,0:T(8,128)(2,1)}) %reduce-scatter.6.cloned.1.call-update) | async-done | bytes 557072 | tf_op jit(solution)/shard_map/reduce_scatter | solution.py:310
  618.7 12.4 %collective-permute-done.19 = bf16[512,512]{1,0:T(8,128)(2,1)} collective-permute-done((bf16[512,512]{1,0:T(8,128)(2,1)}, bf16[512,512]{1,0:T(8,128)(2,1)}, u32[]{:S(2)}, u32[]{:S(2)}) %collective-permute-start.19) | collective-permute-done | bytes 524320 | tf_op jit(solution)/shard_map/ppermute | solution.py:280
  643.5 23.2 %collective-permute-done.25 = bf16[1024,512]{1,0:T(8,128)(2,1)} collective-permute-done((bf16[1024,512]{1,0:T(8,128)(2,1)}, bf16[1024,512]{1,0:T(8,128)(2,1)}, u32[]{:S(2)}, u32[]{:S(2)}) %collective-permute-start.25) | collective-permute-done | bytes 1048608 | tf_op jit(solution)/shard_map/ppermute | solution.py:280
  677.4 15.5 %bitcast_convert_fusion.1 = bf16[512,2048]{1,0:T(8,128)(2,1)} fusion(bf16[2,8,256,512]{3,2,1,0:T(8,128)(2,1)} %get-tuple-element.88, bf16[2,8,256,2048]{3,2,1,0:T(8,128)(2,1)} %get-tuple-element.80), kind=kOutput, calls=%fused_computation.19 | convolution fusion | flops 8590983168 | bytes 23068672 | tf_op jit(solution)/shard_map/dot_general | solution.py:21
  704.1 16.0 %shard_map.264 = (f32[1024,512]{1,0:T(8,128)}, f32[1024,512]{1,0:T(8,128)}, bf16[1024,512]{1,0:T(8,128)(2,1)}) custom-call(s32[1]{0:T(128)} %copy.289.length, bf16[1024,512]{1,0:T(8,128)(2,1)} %bitcast.322, bf16[1024,512]{1,0:T(8,128)(2,1)} %bitcast.324, bf16[1024,512]{1,0:T(8,128)(2,1)} %convolution_convert_fusion.5.v_ref, ...), custom_call_target="tpu_custom_call" | custom-call | tf_op jit(solution)/shard_map/pallas_call | solution.py:106
  726.0 6.0 multiply_add_fusion.1
  744.8 86.4 %collective-permute-done.28 = f32[2,1024]{1,0:T(2,128)S(1)} collective-permute-done((f32[2,1024]{1,0:T(2,128)S(1)}, f32[2,1024]{1,0:T(2,128)S(1)}, u32[]{:S(2)}, u32[]{:S(2)}) %collective-permute-start.28) | collective-permute-done | bytes 8224 | tf_op jit(solution)/shard_map/ppermute | solution.py:280
  856.7 24.6 %collective-permute-done.50 = bf16[4,256,512]{2,1,0:T(8,128)(2,1)S(1)} collective-permute-done((bf16[4,256,512]{2,1,0:T(8,128)(2,1)S(1)}, bf16[4,256,512]{2,1,0:T(8,128)(2,1)S(1)}, u32[]{:S(2)}, u32[]{:S(2)}) %collective-permute-start.50) | collective-permute-done | bytes 1048608 | tf_op jit(solution)/shard_map/ppermute | solution.py:283
  885.5 29.0 %collective-permute-done.39 = bf16[4,256,512]{2,1,0:T(8,128)(2,1)S(1)} collective-permute-done((bf16[4,256,512]{2,1,0:T(8,128)(2,1)S(1)}, bf16[4,256,512]{2,1,0:T(8,128)(2,1)S(1)}, u32[]{:S(2)}, u32[]{:S(2)}) %collective-permute-start.39) | collective-permute-done | bytes 1048608 | tf_op jit(solution)/shard_map/ppermute | solution.py:283
  917.4 12.1 %collective-permute-done.51 = bf16[256,512]{1,0:T(8,128)(2,1)S(1)} collective-permute-done((bf16[256,512]{1,0:T(8,128)(2,1)S(1)}, bf16[256,512]{1,0:T(8,128)(2,1)S(1)}, u32[]{:S(2)}, u32[]{:S(2)}) %collective-permute-start.51) | collective-permute-done | bytes 262176 | tf_op jit(solution)/shard_map/ppermute | solution.py:286
  930.5 8.9 collective-permute-done.40
  939.4 7.7 collective-permute-start.63
  950.4 6.9 convert_add_fusion
  957.3 11.7 %reshape.308 = f32[2048,2,2,256]{3,2,1,0:T(2,128)} reshape(f32[2048,1024]{1,0:T(8,128)} %convert_add_fusion) | data formatting | bytes 16777216 | tf_op jit(solution)/shard_map/reshape | solution.py:571
  969.0 5.6 fusion.129
  1022.1 5.3 copy.205
  1032.6 5.7 collective-permute-done.66
  1044.6 5.0 collective-permute-done.44
  1050.4 4.8 collective-permute-done.67
  1061.4 4.6 collective-permute-done.45
  1069.1 6.9 collective-permute-done.56
  1091.4 15.1 %collective-permute-done.46 = bf16[256,512]{1,0:T(8,128)(2,1)S(1)} collective-permute-done((bf16[256,512]{1,0:T(8,128)(2,1)S(1)}, bf16[256,512]{1,0:T(8,128)(2,1)S(1)}, u32[]{:S(2)}, u32[]{:S(2)}) %collective-permute-start.46) | collective-permute-done | bytes 262176 | tf_op jit(solution)/shard_map/ppermute | solution.py:283
  1109.4 13.6 %collective-permute-done.57 = bf16[256,512]{1,0:T(8,128)(2,1)S(1)} collective-permute-done((bf16[256,512]{1,0:T(8,128)(2,1)S(1)}, bf16[256,512]{1,0:T(8,128)(2,1)S(1)}, u32[]{:S(2)}, u32[]{:S(2)}) %collective-permute-start.57) | collective-permute-done | bytes 262176 | tf_op jit(solution)/shard_map/ppermute | solution.py:283
  1133.7 4.8 collective-permute-done.18
  (496 shorter events, 297.3 us)
Async XLA Ops:
  7.2 39.6 %all-gather.9.cloned.1.call-start = ((), (), s32[]{:S(2)}) async-start(), calls=%async_computation.3 | async-start | bytes 5242880 | tf_op jit(solution)/shard_map/all_gather | solution.py:356
  7.9 178.8 %all-gather.11.cloned.1.call-start = ((), (), s32[]{:S(2)}) async-start(), calls=%async_computation.8 | async-start | bytes 9437184 | tf_op jit(solution)/shard_map/all_gather | solution.py:364
  62.1 206.4 %all-gather.13.cloned.1.call-start = ((), (), s32[]{:S(2)}) async-start(), calls=%async_computation.9 | async-start | bytes 4718592 | tf_op jit(solution)/shard_map/all_gather | solution.py:401
  134.2 25.5 %collective-permute-start.4 = (bf16[1024,512]{1,0:T(8,128)(2,1)}, bf16[1024,512]{1,0:T(8,128)(2,1)}, u32[]{:S(2)}, u32[]{:S(2)}) collective-permute-start(bf16[1024,512]{1,0:T(8,128)(2,1)} %add_convert_fusion.8), channel_id=1, source_target_pairs={{0,2},{1,3},{2,0},{3,1},{4,6},{5,7},{6,4},{7,5},{8,10},{9,11},{10,... | collective-permute-start | bytes 3145736 | tf_op jit(solution)/shard_map/ppermute | solution.py:280
  189.0 222.2 %all-gather.15.cloned.1.call-start = ((), (), s32[]{:S(2)}) async-start(), calls=%async_computation.10 | async-start | bytes 4718592 | tf_op jit(solution)/shard_map/all_gather | solution.py:401
  189.0 153.4 %collective-permute-start.10 = (bf16[8,2,512,512]{3,2,1,0:T(8,128)(2,1)}, bf16[8,2,512,512]{3,2,1,0:T(8,128)(2,1)}, u32[]{:S(2)}, u32[]{:S(2)}) collective-permute-start(bf16[8,2,512,512]{3,2,1,0:T(8,128)(2,1)} %bitcast.311), channel_id=1, source_target_pairs={{0,1},{1,0},{2,3},{3,2},{4,5},{5,4},{6,7},{7,6},{8,9},{9,8},{10,11... | collective-permute-start | bytes 25165832 | tf_op jit(solution)/shard_map/ppermute | solution.py:277
  204.1 138.3 %collective-permute-start.11 = (bf16[2048,1024]{1,0:T(8,128)(2,1)}, bf16[2048,1024]{1,0:T(8,128)(2,1)}, u32[]{:S(2)}, u32[]{:S(2)}) collective-permute-start(bf16[2048,1024]{1,0:T(8,128)(2,1)} %pad_maximum_fusion.2.gate_up_own), channel_id=1, source_target_pairs={{0,2},{1,3},{2,0},{3,1},{4,6},{5,7},{6,4},{7,5},{8,10},{9,11},{10,... | collective-permute-start | bytes 12582920 | tf_op jit(solution)/shard_map/ppermute | solution.py:280
  268.4 74.0 %collective-permute-start.9 = (bf16[8,2,256,512]{3,2,1,0:T(8,128)(2,1)}, bf16[8,2,256,512]{3,2,1,0:T(8,128)(2,1)}, u32[]{:S(2)}, u32[]{:S(2)}) collective-permute-start(bf16[8,2,256,512]{3,2,1,0:T(8,128)(2,1)} %bitcast.332), channel_id=1, source_target_pairs={{0,1},{1,0},{2,3},{3,2},{4,5},{5,4},{6,7},{7,6},{8,9},{9,8},{10,11... | collective-permute-start | bytes 12582920 | tf_op jit(solution)/shard_map/ppermute | solution.py:277
  268.5 306.0 %reduce-scatter.4.cloned.1.call-start = ((), (), s32[]{:S(2)}) async-start(), calls=%async_computation.4 | async-start | bytes 5013504 | tf_op jit(solution)/shard_map/reduce_scatter | solution.py:310
  268.7 73.7 %collective-permute-start.12 = (bf16[512,2048]{1,0:T(8,128)(2,1)}, bf16[512,2048]{1,0:T(8,128)(2,1)}, u32[]{:S(2)}, u32[]{:S(2)}) collective-permute-start(bf16[512,2048]{1,0:T(8,128)(2,1)} %bitcast.326), channel_id=1, source_target_pairs={{0,2},{1,3},{2,0},{3,1},{4,6},{5,7},{6,4},{7,5},{8,10},{9,11},{10,... | collective-permute-start | bytes 6291464 | tf_op jit(solution)/shard_map/ppermute | solution.py:280
  411.1 15.0 %collective-permute-start.14 = (bf16[8,2,256,512]{3,2,1,0:T(8,128)(2,1)}, bf16[8,2,256,512]{3,2,1,0:T(8,128)(2,1)}, u32[]{:S(2)}, u32[]{:S(2)}) collective-permute-start(bf16[8,2,256,512]{3,2,1,0:T(8,128)(2,1)} %bitcast.343), channel_id=1, source_target_pairs={{0,1},{1,0},{2,3},{3,2},{4,5},{5,4},{6,7},{7,6},{8,9},{9,8},{10,11... | collective-permute-start | bytes 12582920 | tf_op jit(solution)/shard_map/ppermute | solution.py:277
  425.7 185.6 %reduce-scatter.6.cloned.1.call-start = ((), (), s32[]{:S(2)}) async-start(), calls=%async_computation.5 | async-start | bytes 5013504 | tf_op jit(solution)/shard_map/reduce_scatter | solution.py:310
  477.6 77.9 %collective-permute-start.16 = (bf16[8,2,256,512]{3,2,1,0:T(8,128)(2,1)}, bf16[8,2,256,512]{3,2,1,0:T(8,128)(2,1)}, u32[]{:S(2)}, u32[]{:S(2)}) collective-permute-start(bf16[8,2,256,512]{3,2,1,0:T(8,128)(2,1)} %get-tuple-element.73), channel_id=1, source_target_pairs={{0,1},{1,0},{2,3},{3,2},{4,5},{5,4},{6,7},{7,6},{8,9},{9,8},{10,11... | collective-permute-start | bytes 12582920 | tf_op jit(solution)/shard_map/ppermute | solution.py:277
  481.8 79.5 %collective-permute-start.17 = (bf16[8,2,256,512]{3,2,1,0:T(8,128)(2,1)}, bf16[8,2,256,512]{3,2,1,0:T(8,128)(2,1)}, u32[]{:S(2)}, u32[]{:S(2)}) collective-permute-start(bf16[8,2,256,512]{3,2,1,0:T(8,128)(2,1)} %get-tuple-element.75), channel_id=1, source_target_pairs={{0,1},{1,0},{2,3},{3,2},{4,5},{5,4},{6,7},{7,6},{8,9},{9,8},{10,11... | collective-permute-start | bytes 12582920 | tf_op jit(solution)/shard_map/ppermute | solution.py:277
  492.1 518.6 %all-reduce.4.cloned.1.call-start = ((), (), s32[]{:S(2)}) async-start(), calls=%async_computation.7 | async-start | bytes 4194304 | tf_op jit(solution)/shard_map/psum | solution.py:557
  642.3 24.4 %collective-permute-start.25 = (bf16[1024,512]{1,0:T(8,128)(2,1)}, bf16[1024,512]{1,0:T(8,128)(2,1)}, u32[]{:S(2)}, u32[]{:S(2)}) collective-permute-start(bf16[1024,512]{1,0:T(8,128)(2,1)} %fusion.118), channel_id=1, source_target_pairs={{0,2},{1,3},{2,0},{3,1},{4,6},{5,7},{6,4},{7,5},{8,10},{9,11},{10,... | collective-permute-start | bytes 3145736 | tf_op jit(solution)/shard_map/ppermute | solution.py:280
  643.5 27.7 %collective-permute-start.24 = (bf16[1024,512]{1,0:T(8,128)(2,1)}, bf16[1024,512]{1,0:T(8,128)(2,1)}, u32[]{:S(2)}, u32[]{:S(2)}) collective-permute-start(bf16[1024,512]{1,0:T(8,128)(2,1)} %fusion.118), channel_id=1, source_target_pairs={{0,1},{1,0},{2,3},{3,2},{4,5},{5,4},{6,7},{7,6},{8,9},{9,8},{10,11... | collective-permute-start | bytes 3145736 | tf_op jit(solution)/shard_map/ppermute | solution.py:277
  676.7 450.5 %reduce-scatter.8.cloned.1.call-start = ((), (), s32[]{:S(2)}) async-start(), calls=%async_computation.6 | async-start | bytes 9437184 | tf_op jit(solution)/shard_map/reduce_scatter | solution.py:310
  692.9 255.0 %collective-permute-start.73 = (bf16[512,2048]{1,0:T(8,128)(2,1)}, bf16[512,2048]{1,0:T(8,128)(2,1)}, u32[]{:S(2)}, u32[]{:S(2)}) collective-permute-start(bf16[512,2048]{1,0:T(8,128)(2,1)} %bitcast_convert_fusion.1), channel_id=1, source_target_pairs={{0,2},{1,3},{2,0},{3,1},{4,6},{5,7},{6,4},{7,5},{8,10},{9,11},{10,... | collective-permute-start | bytes 6291464 | tf_op jit(solution)/shard_map/ppermute | solution.py:280
  693.6 256.8 %collective-permute-start.72 = (bf16[2048,1024]{1,0:T(8,128)(2,1)}, bf16[2048,1024]{1,0:T(8,128)(2,1)}, u32[]{:S(2)}, u32[]{:S(2)}) collective-permute-start(bf16[2048,1024]{1,0:T(8,128)(2,1)} %bitcast_convert_fusion), channel_id=1, source_target_pairs={{0,2},{1,3},{2,0},{3,1},{4,6},{5,7},{6,4},{7,5},{8,10},{9,11},{10,... | collective-permute-start | bytes 12582920 | tf_op jit(solution)/shard_map/ppermute | solution.py:280
  742.4 88.8 %collective-permute-start.28 = (f32[2,1024]{1,0:T(2,128)S(1)}, f32[2,1024]{1,0:T(2,128)S(1)}, u32[]{:S(2)}, u32[]{:S(2)}) collective-permute-start(f32[2,1024]{1,0:T(2,128)S(1)} %fusion.115), channel_id=1, source_target_pairs={{0,2},{1,3},{2,0},{3,1},{4,6},{5,7},{6,4},{7,5},{8,10},{9,11},{10,... | collective-permute-start | bytes 24584 | tf_op jit(solution)/shard_map/ppermute | solution.py:280
  743.3 112.4 %collective-permute-start.61 = (bf16[4,256,512]{2,1,0:T(8,128)(2,1)S(1)}, bf16[4,256,512]{2,1,0:T(8,128)(2,1)S(1)}, u32[]{:S(2)}, u32[]{:S(2)}) collective-permute-start(bf16[4,256,512]{2,1,0:T(8,128)(2,1)S(1)} %dynamic-slice_bitcast_fusion), channel_id=1, source_target_pairs={{0,4},{4,0},{8,12},{12,8},{16,20},{20,16},{24,28},{28,24},{1,5},{5... | collective-permute-start | bytes 3145736 | tf_op jit(solution)/shard_map/ppermute | solution.py:283
  844.0 37.3 %collective-permute-start.50 = (bf16[4,256,512]{2,1,0:T(8,128)(2,1)S(1)}, bf16[4,256,512]{2,1,0:T(8,128)(2,1)S(1)}, u32[]{:S(2)}, u32[]{:S(2)}) collective-permute-start(bf16[4,256,512]{2,1,0:T(8,128)(2,1)S(1)} %dynamic-slice_bitcast_fusion.1), channel_id=1, source_target_pairs={{0,4},{4,0},{8,12},{12,8},{16,20},{20,16},{24,28},{28,24},{1,5},{5... | collective-permute-start | bytes 3145736 | tf_op jit(solution)/shard_map/ppermute | solution.py:283
  855.7 26.1 %collective-permute-start.30 = (bf16[1024,512]{1,0:T(8,128)(2,1)S(1)}, bf16[1024,512]{1,0:T(8,128)(2,1)S(1)}, u32[]{:S(2)}, u32[]{:S(2)}) collective-permute-start(bf16[1024,512]{1,0:T(8,128)(2,1)S(1)} %add_convert_fusion.5), channel_id=1, source_target_pairs={{0,1},{1,0},{2,3},{3,2},{4,5},{5,4},{6,7},{7,6},{8,9},{9,8},{10,11... | collective-permute-start | bytes 3145736 | tf_op jit(solution)/shard_map/ppermute | solution.py:277
  855.7 58.9 %collective-permute-start.39 = (bf16[4,256,512]{2,1,0:T(8,128)(2,1)S(1)}, bf16[4,256,512]{2,1,0:T(8,128)(2,1)S(1)}, u32[]{:S(2)}, u32[]{:S(2)}) collective-permute-start(bf16[4,256,512]{2,1,0:T(8,128)(2,1)S(1)} %dynamic-slice_bitcast_fusion.2), channel_id=1, source_target_pairs={{0,4},{4,0},{8,12},{12,8},{16,20},{20,16},{24,28},{28,24},{1,5},{5... | collective-permute-start | bytes 3145736 | tf_op jit(solution)/shard_map/ppermute | solution.py:283
  881.3 117.4 %collective-permute-start.29 = (bf16[1024,512]{1,0:T(8,128)(2,1)}, bf16[1024,512]{1,0:T(8,128)(2,1)}, u32[]{:S(2)}, u32[]{:S(2)}) collective-permute-start(bf16[1024,512]{1,0:T(8,128)(2,1)} %add_convert_fusion.6), channel_id=1, source_target_pairs={{0,1},{1,0},{2,3},{3,2},{4,5},{5,4},{6,7},{7,6},{8,9},{9,8},{10,11... | collective-permute-start | bytes 3145736 | tf_op jit(solution)/shard_map/ppermute | solution.py:277
  881.7 34.9 %collective-permute-start.62 = (bf16[256,512]{1,0:T(8,128)(2,1)S(1)}, bf16[256,512]{1,0:T(8,128)(2,1)S(1)}, u32[]{:S(2)}, u32[]{:S(2)}) collective-permute-start(bf16[256,512]{1,0:T(8,128)(2,1)S(1)} %fusion.76), channel_id=1, source_target_pairs={{0,8},{4,12},{8,16},{12,20},{16,24},{20,28},{24,0},{28,4},{1,9},{5... | collective-permute-start | bytes 786440 | tf_op jit(solution)/shard_map/ppermute | solution.py:286
  914.6 14.9 %collective-permute-start.51 = (bf16[256,512]{1,0:T(8,128)(2,1)S(1)}, bf16[256,512]{1,0:T(8,128)(2,1)S(1)}, u32[]{:S(2)}, u32[]{:S(2)}) collective-permute-start(bf16[256,512]{1,0:T(8,128)(2,1)S(1)} %fusion.75), channel_id=1, source_target_pairs={{0,8},{4,12},{8,16},{12,20},{16,24},{20,28},{24,0},{28,4},{1,9},{5... | collective-permute-start | bytes 786440 | tf_op jit(solution)/shard_map/ppermute | solution.py:286
  916.6 22.8 %collective-permute-start.40 = (bf16[256,512]{1,0:T(8,128)(2,1)S(1)}, bf16[256,512]{1,0:T(8,128)(2,1)S(1)}, u32[]{:S(2)}, u32[]{:S(2)}) collective-permute-start(bf16[256,512]{1,0:T(8,128)(2,1)S(1)} %fusion.74), channel_id=1, source_target_pairs={{0,8},{4,12},{8,16},{12,20},{16,24},{20,28},{24,0},{28,4},{1,9},{5... | collective-permute-start | bytes 786440 | tf_op jit(solution)/shard_map/ppermute | solution.py:286
  929.5 69.2 %collective-permute-start.31 = (bf16[1024,512]{1,0:T(8,128)(2,1)}, bf16[1024,512]{1,0:T(8,128)(2,1)}, u32[]{:S(2)}, u32[]{:S(2)}) collective-permute-start(bf16[1024,512]{1,0:T(8,128)(2,1)} %add_convert_fusion.4), channel_id=1, source_target_pairs={{0,2},{1,3},{2,0},{3,1},{4,6},{5,7},{6,4},{7,5},{8,10},{9,11},{10,... | collective-permute-start | bytes 3145736 | tf_op jit(solution)/shard_map/ppermute | solution.py:280
  939.4 44.4 %collective-permute-start.63 = (bf16[256,512]{1,0:T(8,128)(2,1)S(1)}, bf16[256,512]{1,0:T(8,128)(2,1)}, u32[]{:S(2)}, u32[]{:S(2)}) collective-permute-start(bf16[256,512]{1,0:T(8,128)(2,1)S(1)} %fusion.24), channel_id=1, source_target_pairs={{0,8},{4,12},{8,16},{12,20},{16,24},{20,28},{24,0},{28,4},{1,9},{5... | collective-permute-start | bytes 786440 | tf_op jit(solution)/shard_map/ppermute | solution.py:286
  947.9 37.8 %collective-permute-start.52 = (bf16[256,512]{1,0:T(8,128)(2,1)}, bf16[256,512]{1,0:T(8,128)(2,1)}, u32[]{:S(2)}, u32[]{:S(2)}) collective-permute-start(bf16[256,512]{1,0:T(8,128)(2,1)} %fusion.27), channel_id=1, source_target_pairs={{0,8},{4,12},{8,16},{12,20},{16,24},{20,28},{24,0},{28,4},{1,9},{5... | collective-permute-start | bytes 786440 | tf_op jit(solution)/shard_map/ppermute | solution.py:286
  950.4 39.6 %collective-permute-start.41 = (bf16[256,512]{1,0:T(8,128)(2,1)}, bf16[256,512]{1,0:T(8,128)(2,1)}, u32[]{:S(2)}, u32[]{:S(2)}) collective-permute-start(bf16[256,512]{1,0:T(8,128)(2,1)} %fusion.30), channel_id=1, source_target_pairs={{0,8},{4,12},{8,16},{12,20},{16,24},{20,28},{24,0},{28,4},{1,9},{5... | collective-permute-start | bytes 786440 | tf_op jit(solution)/shard_map/ppermute | solution.py:286
  987.6 15.1 %collective-permute-start.53 = (bf16[256,512]{1,0:T(8,128)(2,1)}, bf16[256,512]{1,0:T(8,128)(2,1)}, u32[]{:S(2)}, u32[]{:S(2)}) collective-permute-start(bf16[256,512]{1,0:T(8,128)(2,1)} %fusion.28), channel_id=1, source_target_pairs={{0,8},{4,12},{8,16},{12,20},{16,24},{20,28},{24,0},{28,4},{1,9},{5... | collective-permute-start | bytes 786440 | tf_op jit(solution)/shard_map/ppermute | solution.py:286
  991.8 15.6 %collective-permute-start.42 = (bf16[256,512]{1,0:T(8,128)(2,1)}, bf16[256,512]{1,0:T(8,128)(2,1)}, u32[]{:S(2)}, u32[]{:S(2)}) collective-permute-start(bf16[256,512]{1,0:T(8,128)(2,1)} %fusion.31), channel_id=1, source_target_pairs={{0,8},{4,12},{8,16},{12,20},{16,24},{20,28},{24,0},{28,4},{1,9},{5... | collective-permute-start | bytes 786440 | tf_op jit(solution)/shard_map/ppermute | solution.py:286
  996.8 89.0 %collective-permute-start.71 = (bf16[256,512]{1,0:T(8,128)(2,1)}, bf16[256,512]{1,0:T(8,128)(2,1)}, u32[]{:S(2)}, u32[]{:S(2)}) collective-permute-start(bf16[256,512]{1,0:T(8,128)(2,1)} %fusion.26), channel_id=1, source_target_pairs={{0,4},{4,0},{8,12},{12,8},{16,20},{20,16},{24,28},{28,24},{1,5},{5... | collective-permute-start | bytes 786440 | tf_op jit(solution)/shard_map/ppermute | solution.py:283
  998.7 28.7 %collective-permute-start.65 = (bf16[256,512]{1,0:T(8,128)(2,1)}, bf16[256,512]{1,0:T(8,128)(2,1)S(1)}, u32[]{:S(2)}, u32[]{:S(2)}) collective-permute-start(bf16[256,512]{1,0:T(8,128)(2,1)} %fusion.26), channel_id=1, source_target_pairs={{0,8},{4,12},{8,16},{12,20},{16,24},{20,28},{24,0},{28,4},{1,9},{5... | collective-permute-start | bytes 786440 | tf_op jit(solution)/shard_map/ppermute | solution.py:286
  1004.6 118.5 %collective-permute-start.60 = (bf16[256,512]{1,0:T(8,128)(2,1)}, bf16[256,512]{1,0:T(8,128)(2,1)}, u32[]{:S(2)}, u32[]{:S(2)}) collective-permute-start(bf16[256,512]{1,0:T(8,128)(2,1)} %fusion.29), channel_id=1, source_target_pairs={{0,4},{4,0},{8,12},{12,8},{16,20},{20,16},{24,28},{28,24},{1,5},{5... | collective-permute-start | bytes 786440 | tf_op jit(solution)/shard_map/ppermute | solution.py:283
  1009.4 23.2 %collective-permute-start.43 = (bf16[256,512]{1,0:T(8,128)(2,1)}, bf16[256,512]{1,0:T(8,128)(2,1)}, u32[]{:S(2)}, u32[]{:S(2)}) collective-permute-start(bf16[256,512]{1,0:T(8,128)(2,1)} %fusion.32), channel_id=1, source_target_pairs={{0,8},{4,12},{8,16},{12,20},{16,24},{20,28},{24,0},{28,4},{1,9},{5... | collective-permute-start | bytes 786440 | tf_op jit(solution)/shard_map/ppermute | solution.py:286
  1039.2 16.1 %collective-permute-start.67 = (bf16[256,512]{1,0:T(8,128)(2,1)S(1)}, bf16[256,512]{1,0:T(8,128)(2,1)S(1)}, u32[]{:S(2)}, u32[]{:S(2)}) collective-permute-start(bf16[256,512]{1,0:T(8,128)(2,1)S(1)} %collective-permute-done.66), channel_id=1, source_target_pairs={{0,8},{4,12},{8,16},{12,20},{16,24},{20,28},{24,0},{28,4},{1,9},{5... | collective-permute-start | bytes 786440 | tf_op jit(solution)/shard_map/ppermute | solution.py:286
  1044.0 41.1 %collective-permute-start.70 = (bf16[256,512]{1,0:T(8,128)(2,1)S(1)}, bf16[256,512]{1,0:T(8,128)(2,1)S(1)}, u32[]{:S(2)}, u32[]{:S(2)}) collective-permute-start(bf16[256,512]{1,0:T(8,128)(2,1)S(1)} %collective-permute-done.65), channel_id=1, source_target_pairs={{0,4},{4,0},{8,12},{12,8},{16,20},{20,16},{24,28},{28,24},{1,5},{5... | collective-permute-start | bytes 786440 | tf_op jit(solution)/shard_map/ppermute | solution.py:283
  1060.8 22.7 %collective-permute-start.69 = (bf16[256,512]{1,0:T(8,128)(2,1)S(1)}, bf16[256,512]{1,0:T(8,128)(2,1)S(1)}, u32[]{:S(2)}, u32[]{:S(2)}) collective-permute-start(bf16[256,512]{1,0:T(8,128)(2,1)S(1)} %collective-permute-done.66), channel_id=1, source_target_pairs={{0,4},{4,0},{8,12},{12,8},{16,20},{20,16},{24,28},{28,24},{1,5},{5... | collective-permute-start | bytes 786440 | tf_op jit(solution)/shard_map/ppermute | solution.py:283
  1082.9 26.4 %collective-permute-start.49 = (bf16[256,512]{1,0:T(8,128)(2,1)}, bf16[256,512]{1,0:T(8,128)(2,1)S(1)}, u32[]{:S(2)}, u32[]{:S(2)}) collective-permute-start(bf16[256,512]{1,0:T(8,128)(2,1)} %fusion.32), channel_id=1, source_target_pairs={{0,4},{4,0},{8,12},{12,8},{16,20},{20,16},{24,28},{28,24},{1,5},{5... | collective-permute-start | bytes 786440 | tf_op jit(solution)/shard_map/ppermute | solution.py:283
  1083.6 25.1 %collective-permute-start.48 = (bf16[256,512]{1,0:T(8,128)(2,1)}, bf16[256,512]{1,0:T(8,128)(2,1)S(1)}, u32[]{:S(2)}, u32[]{:S(2)}) collective-permute-start(bf16[256,512]{1,0:T(8,128)(2,1)} %collective-permute-done.43), channel_id=1, source_target_pairs={{0,4},{4,0},{8,12},{12,8},{16,20},{20,16},{24,28},{28,24},{1,5},{5... | collective-permute-start | bytes 786440 | tf_op jit(solution)/shard_map/ppermute | solution.py:283
  1085.1 22.0 %collective-permute-start.47 = (bf16[256,512]{1,0:T(8,128)(2,1)S(1)}, bf16[256,512]{1,0:T(8,128)(2,1)S(1)}, u32[]{:S(2)}, u32[]{:S(2)}) collective-permute-start(bf16[256,512]{1,0:T(8,128)(2,1)S(1)} %collective-permute-done.44), channel_id=1, source_target_pairs={{0,4},{4,0},{8,12},{12,8},{16,20},{20,16},{24,28},{28,24},{1,5},{5... | collective-permute-start | bytes 786440 | tf_op jit(solution)/shard_map/ppermute | solution.py:283
  1085.8 20.7 %collective-permute-start.46 = (bf16[256,512]{1,0:T(8,128)(2,1)S(1)}, bf16[256,512]{1,0:T(8,128)(2,1)S(1)}, u32[]{:S(2)}, u32[]{:S(2)}) collective-permute-start(bf16[256,512]{1,0:T(8,128)(2,1)S(1)} %collective-permute-done.45), channel_id=1, source_target_pairs={{0,4},{4,0},{8,12},{12,8},{16,20},{20,16},{24,28},{28,24},{1,5},{5... | collective-permute-start | bytes 786440 | tf_op jit(solution)/shard_map/ppermute | solution.py:283
  1106.5 16.6 %collective-permute-start.59 = (bf16[256,512]{1,0:T(8,128)(2,1)S(1)}, bf16[256,512]{1,0:T(8,128)(2,1)S(1)}, u32[]{:S(2)}, u32[]{:S(2)}) collective-permute-start(bf16[256,512]{1,0:T(8,128)(2,1)S(1)} %collective-permute-done.54), channel_id=1, source_target_pairs={{0,4},{4,0},{8,12},{12,8},{16,20},{20,16},{24,28},{28,24},{1,5},{5... | collective-permute-start | bytes 786440 | tf_op jit(solution)/shard_map/ppermute | solution.py:283
  1107.1 15.9 %collective-permute-start.58 = (bf16[256,512]{1,0:T(8,128)(2,1)S(1)}, bf16[256,512]{1,0:T(8,128)(2,1)S(1)}, u32[]{:S(2)}, u32[]{:S(2)}) collective-permute-start(bf16[256,512]{1,0:T(8,128)(2,1)S(1)} %collective-permute-done.55), channel_id=1, source_target_pairs={{0,4},{4,0},{8,12},{12,8},{16,20},{20,16},{24,28},{28,24},{1,5},{5... | collective-permute-start | bytes 786440 | tf_op jit(solution)/shard_map/ppermute | solution.py:283
  (95 other events, 1285.8 us)
Sparse Core Ops, SparseCore 0:
  9.6 37.1 all-gather.8
  62.2 124.4 all-gather.10
  189.4 78.9 all-gather.12
  270.4 72.5 all-gather.14
  425.8 90.2 reduce-scatter.3
  519.6 91.7 reduce-scatter.5
  676.8 105.7 all-reduce.3
  786.3 195.2 reduce-scatter.7
